TPU v7x, 512 devices: a whole 4x4x16 slice. The times are simulated.
512 devices in a mesh: flow: 16 (over y_lo, x, core), tm: 32 (over z, y_hi).
Axes of the slice: x: 4, y: 4 (y_hi: 2, y_lo: 2; y = y_hi * 2 + y_lo), z: 16, core: 2. Of those that a mesh axis runs over, the one named last changes fastest.
Arguments:
- frames: bfloat16 [512, 512, 1024], P('tm', 'flow'), may hold values from -6 to 6
- pixel_gain: float32 [512, 1024], P('flow'), may hold values from 0.1 to 1.9
- couple: float32 [512, 1024], P('flow'), may hold values from 0.05 to 0.45
- bin_index: int32 [512, 1024], P('flow'), may hold values from 0 to 31
- pixel_mask: int32 [512, 1024], P('flow'), may hold values 0 or 1
- offsets: int32 [512], P('tm'), may hold values from 0 to 24, as said below
Outputs:
- correlation: float32 [32, 32], P('flow', 'tm')
Inputs may be any that keep to these rules, and one draw needn't show every extreme that they name: The pixels of frame t pair with the pixels offsets[t] rows further along the flow in the later frames; the value 24 occurs in every draw.
All inputs are finite; a program needn't handle non-finite values. No bound on the sum of `pixel_mask` on one device may be relied on, other than what follows from the above.
Results may differ from a plain program's by a relative error of at most 0.0041.
Values may be sent and summed in bfloat16 or wider, within the bound.
No kernel may reach another device: no remote copies, remote signals or barrier semaphores. Data moves between devices by JAX's collectives and lax.ppermute only.
A program may use at most 64 MiB of HBM per device.

v0:
```python
import jax
import jax.numpy as jnp
from jax import lax
from jax.sharding import PartitionSpec as P

LAGS = 32
OFF_MAX = 24
Q = 32


def extended_2(block, sides, width):
    for axis, dim in sides:
        count = lax.axis_size(axis)
        forward = [(i, i + 1) for i in range(count - 1)]
        backward = [(target, source) for source, target in forward]
        low = lax.ppermute(
            lax.slice_in_dim(block, block.shape[dim] - width, None, axis=dim), axis, forward
        )
        high = lax.ppermute(lax.slice_in_dim(block, 0, width, axis=dim), axis, backward)
        block = jnp.concatenate([low, block, high], axis=dim)
    return block


def shifted(block, axis, distance):
    devices = range(lax.axis_size(axis))
    route = [(i - distance, i) for i in devices if i - distance in devices]
    return lax.ppermute(block, axis, route)


def correct_block(frames, pixel_gain, couple, pixel_mask):
    padded = extended_2(frames, (("flow", 1),), 1)
    above_rows = padded[:, :-2].astype(jnp.float32)
    below_rows = padded[:, 2:].astype(jnp.float32)
    signal = frames.astype(jnp.float32)
    mask_float = pixel_mask.astype(jnp.float32)
    return ((pixel_gain * signal + couple * (above_rows + below_rows)) * mask_float).astype(
        jnp.bfloat16
    )


def lag_pieces(sent_block, hop_count):
    pieces = []
    for hop_index in range(1, hop_count + 1):
        pieces.append(shifted(sent_block, "tm", -hop_index))
    return pieces


def lagged_products(current_rows, later_block, offsets, frame_count):
    lead_rows = current_rows.shape[1]
    col_count = current_rows.shape[2]

    def add_group(group_index, running):
        for member in range(8):
            frame_index = group_index * 8 + member
            current = lax.dynamic_index_in_dim(current_rows, frame_index, 0, keepdims=False).astype(
                jnp.float32
            )
            window = lax.dynamic_slice(
                later_block,
                (frame_index + 1, offsets[frame_index], 0),
                (LAGS, lead_rows, col_count),
            )
            running = running + current[None] * window.astype(jnp.float32)
        return running

    return lax.fori_loop(
        0, frame_count // 8, add_group, jnp.zeros((LAGS, lead_rows, col_count), jnp.float32)
    )


def binned(running, bins):
    lag_count = running.shape[0]
    bin_table = (bins.reshape(-1)[:, None] == jnp.arange(Q, dtype=jnp.int32)[None, :]).astype(
        jnp.float32
    )
    return jnp.dot(running.reshape(lag_count, -1), bin_table, precision=lax.Precision.HIGHEST).T


def per_device(frames, pixel_gain, couple, bin_index, pixel_mask, offsets):
    frame_count = frames.shape[0]
    row_count = frames.shape[1]
    col_count = frames.shape[2]
    corrected = correct_block(frames, pixel_gain, couple, pixel_mask)
    hop_count = max(1, LAGS // frame_count)
    pieces = lag_pieces(corrected, hop_count)
    extended = jnp.concatenate([corrected] + pieces, axis=0)
    lower_rows = shifted(extended[:, :OFF_MAX], "flow", -1)
    full_block = jnp.concatenate([extended, lower_rows], axis=1)
    running = lagged_products(corrected, full_block, offsets, frame_count)
    partial_sums = binned(running, bin_index)
    flow_count = lax.axis_size("flow")
    time_count = lax.axis_size("tm")
    bin_share = Q // flow_count
    lag_share = LAGS // time_count
    total_sums = lax.psum(partial_sums, ("flow", "tm"))
    owned_block = lax.dynamic_slice(
        total_sums,
        (lax.axis_index("flow") * bin_share, lax.axis_index("tm") * lag_share),
        (bin_share, lag_share),
    )
    frames_total = frame_count * time_count
    rows_total = row_count * flow_count
    lag_values = (
        lax.axis_index("tm") * lag_share + jnp.arange(lag_share, dtype=jnp.int32) + 1
    ).astype(jnp.float32)
    normaliser = jnp.sqrt((frames_total - lag_values) * (rows_total * col_count / Q))
    return owned_block / normaliser[None, :]


def solution(mesh):
    in_specs = (
        P("tm", "flow", None),
        P("flow", None),
        P("flow", None),
        P("flow", None),
        P("flow", None),
        P("tm"),
    )
    out_specs = P("flow", "tm")
    return jax.shard_map(
        per_device, mesh=mesh, in_specs=in_specs, out_specs=out_specs, check_vma=False
    )
```

profile of v0, /device:TPU:1, one launch (start us, length us, event | category | flops | bytes accessed | tf_op | source)
XLA Modules:
  0.0 287.8 jit_solution(14286662003903903884)
XLA Ops:
  0.0 1.1 fusion.10
  1.1 4.5 %collective-permute-start = (bf16[16,1,1024]{2,1,0:T(2,128)(2,1)S(1)}, bf16[16,1,1024]{2,1,0:T(2,128)(2,1)S(1)}, u32[]{:S(2)}, u32[]{:S(2)}) collective-permute-start(bf16[16,1,1024]{2,1,0:T(2,128)(2,1)S(1)} %get-tuple-element.240), channel_id=1, source_target_pairs={{0,32},{32,64},{64,96},{96,128},{128,160},{160,192},{192,224},{224... | collective-permute-start | bytes 98312 | tf_op jit(solution)/shard_map/ppermute | solution.py:16
  5.6 0.0 copy-start.1
  5.7 5.7 %collective-permute-start.1 = (bf16[16,1,1024]{2,1,0:T(2,128)(2,1)S(1)}, bf16[16,1,1024]{2,1,0:T(2,128)(2,1)S(1)}, u32[]{:S(2)}, u32[]{:S(2)}) collective-permute-start(bf16[16,1,1024]{2,1,0:T(2,128)(2,1)S(1)} %get-tuple-element.241), channel_id=1, source_target_pairs={{32,0},{64,32},{96,64},{128,96},{160,128},{192,160},{224,192},{256... | collective-permute-start | bytes 98312 | tf_op jit(solution)/shard_map/ppermute | solution.py:19
  11.3 0.9 convert_element_type.223
  12.3 0.0 collective-permute-done
  12.3 0.0 collective-permute-done.1
  12.3 3.4 %multiply_convert_fusion = bf16[16,32,1024]{2,1,0:T(8,128)(2,1)S(1)} fusion(bf16[16,32,1024]{2,1,0:T(8,128)(2,1)} %param.8, bf16[16,1,1024]{2,1,0:T(2,128)(2,1)S(1)} %collective-permute-done.1, bf16[16,1,1024]{2,1,0:T(2,128)(2,1)S(1)} %collective-permute-done, f32[32,1024]{1,0:T(8,128)S(1)} %convert_element_type.223, f32[32,1024]{1,0:T(8,128)} %param.10, ...), kind=kLoop, calls=%fused_computation.21 | loop fusion | flops 7864320 | bytes 2555904 | tf_op jit(solution)/shard_map/convert_element_type | solution.py:36
  15.7 1.3 collective-permute-start.2
  17.0 1.3 collective-permute-start.3
  18.3 25.2 %collective-permute-done.2 = bf16[16,32,1024]{2,1,0:T(8,128)(2,1)S(1)} collective-permute-done((bf16[16,32,1024]{2,1,0:T(8,128)(2,1)S(1)}, bf16[16,32,1024]{2,1,0:T(8,128)(2,1)S(1)}, u32[]{:S(2)}, u32[]{:S(2)}) %collective-permute-start.2) | collective-permute-done | bytes 1048608 | tf_op jit(solution)/shard_map/ppermute | solution.py:27
  43.5 21.2 %collective-permute-done.3 = bf16[16,32,1024]{2,1,0:T(8,128)(2,1)S(1)} collective-permute-done((bf16[16,32,1024]{2,1,0:T(8,128)(2,1)S(1)}, bf16[16,32,1024]{2,1,0:T(8,128)(2,1)S(1)}, u32[]{:S(2)}, u32[]{:S(2)}) %collective-permute-start.3) | collective-permute-done | bytes 1048608 | tf_op jit(solution)/shard_map/ppermute | solution.py:27
  64.7 1.7 pad_maximum_fusion.1
  66.4 1.9 collective-permute-start.4
  68.3 0.0 copy-done.1
  68.4 0.0 copy-start
  68.4 29.1 %collective-permute-done.4 = bf16[48,24,1024]{2,1,0:T(8,128)(2,1)} collective-permute-done((bf16[48,24,1024]{2,1,0:T(8,128)(2,1)}, bf16[48,24,1024]{2,1,0:T(8,128)(2,1)}, u32[]{:S(2)}, u32[]{:S(2)}) %collective-permute-start.4) | collective-permute-done | bytes 2359328 | tf_op jit(solution)/shard_map/ppermute | solution.py:27
  97.5 7.4 %pad_maximum_fusion = bf16[48,56,1024]{2,1,0:T(8,128)(2,1)} fusion(bf16[48,24,1024]{2,1,0:T(8,128)(2,1)} %collective-permute-done.4, bf16[16,32,1024]{2,1,0:T(8,128)(2,1)S(1)} %collective-permute-done.3, bf16[16,32,1024]{2,1,0:T(8,128)(2,1)S(1)} %collective-permute-done.2, bf16[16,32,1024]{2,1,0:T(8,128)(2,1)S(1)} %multiply_convert_fusion), kind=kLoop, calls=%fused_computation.16 | loop fusion | flops 22020096 | bytes 11010048 | tf_op jit(solution)/shard_map/concatenate | solution.py:88
  105.0 0.0 copy-done
  105.0 63.4 %while.18 = (s32[]{:T(128)}, f32[32,32,1024]{2,1,0:T(8,128)}, bf16[16,32,1024]{2,1,0:T(8,128)(2,1)S(1)}, s32[16]{0:T(128)S(1)}, bf16[48,56,1024]{2,1,0:T(8,128)(...) while((s32[]{:T(128)}, f32[32,32,1024]{2,1,0:T(8,128)}, ...), condition=%wide.region_1.2_spmd.clone, body=%wide.region_0.1_spmd.clone.sunk | while | flops 26476620 | bytes 27788588 | solution.py:66
  105.0 0.1 bitcast_convert_fusion.9
  105.1 0.7 fusion.14
  120.9 15.4 %fusion.15 = f32[32,32,1024]{2,1,0:T(8,128)} fusion(f32[32,32,1024]{2,1,0:T(8,128)} %get-tuple-element.336, bf16[48,56,1024]{2,1,0:T(8,128)(2,1)} %get-tuple-element.369, s32[]{:T(128)S(6)} %select_n.377, s32[]{:T(128)S(6)} %select_n.386, f32[32,1024]{1,0:T(8,128)S(1)} %get-tuple-element.290, s32[]{:T(128)S(6)} %select_n.387, s32[]{:T(128)S(6)} %select_n.388, ...), kind=kLoop, calls=%fused_computation.7.clone.1 | loop fusion | flops 26214400 | bytes 26214464 | tf_op jit(solution)/shard_map/while/body/eval_jaxpr/add | solution.py:63
  136.3 0.1 bitcast_convert_fusion.9
  136.4 0.7 fusion.14
  152.2 16.2 %fusion.15 = f32[32,32,1024]{2,1,0:T(8,128)} fusion(f32[32,32,1024]{2,1,0:T(8,128)} %get-tuple-element.336, bf16[48,56,1024]{2,1,0:T(8,128)(2,1)} %get-tuple-element.369, s32[]{:T(128)S(6)} %select_n.377, s32[]{:T(128)S(6)} %select_n.386, f32[32,1024]{1,0:T(8,128)S(1)} %get-tuple-element.290, s32[]{:T(128)S(6)} %select_n.387, s32[]{:T(128)S(6)} %select_n.388, ...), kind=kLoop, calls=%fused_computation.7.clone.1 | loop fusion | flops 26214400 | bytes 26214464 | tf_op jit(solution)/shard_map/while/body/eval_jaxpr/add | solution.py:63
  168.3 4.6 %copy.8 = f32[4,8,32,1024]{3,1,2,0:T(8,128)S(1)} copy(f32[4,8,32,1024]{3,2,1,0:T(8,128)} %bitcast.55) | data formatting | bytes 8388608
  173.0 2.6 fusion.7
  175.6 111.6 %psum.7 = f32[32,32]{0,1:T(8,128)S(1)} all-reduce(f32[32,32]{0,1:T(8,128)S(1)} %fusion.7), channel_id=1, replica_groups=mesh['flow'=16,'tm'=32] {'flow','tm'}, use_global_device_ids=true, to_apply=%region_2.3 | all-reduce | flops 1024 | bytes 8192 | tf_op jit(solution)/shard_map/psum | solution.py:95
  287.2 0.6 dynamic-slice_divide_fusion
  (2 shorter events, 0.0 us)
Async XLA Ops:
  1.1 11.1 %collective-permute-start = (bf16[16,1,1024]{2,1,0:T(2,128)(2,1)S(1)}, bf16[16,1,1024]{2,1,0:T(2,128)(2,1)S(1)}, u32[]{:S(2)}, u32[]{:S(2)}) collective-permute-start(bf16[16,1,1024]{2,1,0:T(2,128)(2,1)S(1)} %get-tuple-element.240), channel_id=1, source_target_pairs={{0,32},{32,64},{64,96},{96,128},{128,160},{160,192},{192,224},{224... | collective-permute-start | bytes 98312 | tf_op jit(solution)/shard_map/ppermute | solution.py:16
  5.6 62.7 %copy-start.1 = (s32[32,1024]{1,0:T(8,128)S(1)}, s32[32,1024]{1,0:T(8,128)}, u32[]{:S(2)}) copy-start(s32[32,1024]{1,0:T(8,128)} %param.11) | copy-start | bytes 393220
  5.7 6.6 %collective-permute-start.1 = (bf16[16,1,1024]{2,1,0:T(2,128)(2,1)S(1)}, bf16[16,1,1024]{2,1,0:T(2,128)(2,1)S(1)}, u32[]{:S(2)}, u32[]{:S(2)}) collective-permute-start(bf16[16,1,1024]{2,1,0:T(2,128)(2,1)S(1)} %get-tuple-element.241), channel_id=1, source_target_pairs={{32,0},{64,32},{96,64},{128,96},{160,128},{192,160},{224,192},{256... | collective-permute-start | bytes 98312 | tf_op jit(solution)/shard_map/ppermute | solution.py:19
  15.7 27.8 %collective-permute-start.2 = (bf16[16,32,1024]{2,1,0:T(8,128)(2,1)S(1)}, bf16[16,32,1024]{2,1,0:T(8,128)(2,1)S(1)}, u32[]{:S(2)}, u32[]{:S(2)}) collective-permute-start(bf16[16,32,1024]{2,1,0:T(8,128)(2,1)S(1)} %multiply_convert_fusion), channel_id=1, source_target_pairs={{1,0},{2,1},{3,2},{4,3},{5,4},{6,5},{7,6},{8,7},{9,8},{10,9},{11,1... | collective-permute-start | bytes 3145736 | tf_op jit(solution)/shard_map/ppermute | solution.py:27
  17.0 47.7 %collective-permute-start.3 = (bf16[16,32,1024]{2,1,0:T(8,128)(2,1)S(1)}, bf16[16,32,1024]{2,1,0:T(8,128)(2,1)S(1)}, u32[]{:S(2)}, u32[]{:S(2)}) collective-permute-start(bf16[16,32,1024]{2,1,0:T(8,128)(2,1)S(1)} %multiply_convert_fusion), channel_id=1, source_target_pairs={{2,0},{3,1},{4,2},{5,3},{6,4},{7,5},{8,6},{9,7},{10,8},{11,9},{12,... | collective-permute-start | bytes 3145736 | tf_op jit(solution)/shard_map/ppermute | solution.py:27
  66.4 31.1 %collective-permute-start.4 = (bf16[48,24,1024]{2,1,0:T(8,128)(2,1)}, bf16[48,24,1024]{2,1,0:T(8,128)(2,1)}, u32[]{:S(2)}, u32[]{:S(2)}) collective-permute-start(bf16[48,24,1024]{2,1,0:T(8,128)(2,1)} %pad_maximum_fusion.1), channel_id=1, source_target_pairs={{32,0},{64,32},{96,64},{128,96},{160,128},{192,160},{224,192},{256... | collective-permute-start | bytes 7077896 | tf_op jit(solution)/shard_map/ppermute | solution.py:27
  68.4 36.5 %copy-start = (s32[16]{0:T(128)S(1)}, s32[16]{0:T(128)}, u32[]{:S(2)}) copy-start(s32[16]{0:T(128)} %param.13) | copy-start | bytes 196
where the time goes:
time: 288 us
  blocking collectives  112 us (39%)
  waiting for transfers between devices  75.5 us (26%)
  other arithmetic  45.8 us (16%)
  loops' own time  30.2 us (10%)
  starting transfers between devices  14.7 us (5%)
  local copies, waits for them, and re-layouts  7.2 us (2%)
    psum x1, blocking collectives, per_device(): total_sums = lax.psum(partial_sums, ('flow', 'tm'))  112 us
    ppermute x3, waiting for transfers between devices, shifted(): return lax.ppermute(block, axis, route)  75.5 us
    add x2, other arithmetic, add_group(): running = running + current[None] * window.astype(jnp.float32)  31.6 us
    another operation x1, loops' own time, lagged_products(): lax.fori_loop(0, frame_count // 8, add_group, jnp.zeros((LAGS, lead_rows,...  30.2 us
    concatenate x1, other arithmetic, per_device(): full_block = jnp.concatenate([extended, lower_rows], axis=1)  7.42 us
  transfers between devices with their start and end apart: 5, of which 3 were waited for; matrix products, arithmetic and copies ran while one was open for 0% of the time, Pallas kernels for 0%

commit v1 on v0

v1 whole, which is shorter than its diff:
```python
import jax
import jax.numpy as jnp
from jax import lax
from jax.experimental import pallas as pl
from jax.experimental.pallas import tpu as pltpu
from jax.sharding import PartitionSpec as P

LAGS = 32
OFF_MAX = 24
Q = 32
F32, BF16 = jnp.float32, jnp.bfloat16
VMEM = pl.BlockSpec(memory_space=pltpu.VMEM)
SMEM = pl.BlockSpec(memory_space=pltpu.SMEM)


def correct_kernel(
    h_ref, f_ref, up_ref, dn_ref, gain_ref, couple_ref, mask_ref, o24, o8, t24, t8, raw, done
):
    h = h_ref[0]

    @pl.loop(0, 16)
    def _(f):
        for j in range(8):
            cols = slice(128 * j, 128 * j + 128)
            for k in range(2):
                raw[f, j, 8 + 16 * k : 24 + 16 * k, :] = f_ref[
                    f, 16 * k : 16 * k + 16, cols
                ].astype(F32)

    for f in range(16):
        for j in range(8):
            cols = slice(128 * j, 128 * j + 128)
            raw[f, j, 7:8, :] = up_ref[f : f + 1, cols].astype(F32)
            raw[f, j, 40:41, :] = dn_ref[f : f + 1, cols].astype(F32)

    @pl.loop(0, 16)
    def _(f):
        for j in range(8):
            cols = slice(128 * j, 128 * j + 128)
            for k in range(4):
                rows = slice(8 * k, 8 * k + 8)
                here = raw[f, j, 8 * k + 8 : 8 * k + 16, :]
                above = raw[f, j, 8 * k + 7 : 8 * k + 15, :]
                below = raw[f, j, 8 * k + 9 : 8 * k + 17, :]
                value = gain_ref[rows, cols] * here + couple_ref[rows, cols] * (above + below)
                value = value * mask_ref[rows, cols].astype(F32)
                start = (j // 4) * 2048 + k * 512 + (j % 4) + 4 * f
                done[pl.ds(start, 8, stride=64), :] = value

    own = pl.multiple_of(h * 2048, 2048)
    other = pl.multiple_of(2048 - h * 2048, 2048)

    @pl.loop(0, 24)
    def _(r):
        o24[r] = done[pl.ds(own + r * 64, 64), :].astype(BF16)
        t24[r] = done[pl.ds(other + r * 64, 64), :].astype(BF16)

    @pl.loop(0, 8)
    def _(r):
        o8[r] = done[pl.ds(own + (r + 24) * 64, 64), :].astype(BF16)
        t8[r] = done[pl.ds(other + (r + 24) * 64, 64), :].astype(BF16)


def correct(h, frames, up, dn, gain, couple, mask):
    shapes = tuple(jax.ShapeDtypeStruct((n, 64, 128), BF16) for n in (24, 8, 24, 8))
    return pl.pallas_call(
        correct_kernel,
        out_shape=shapes,
        in_specs=[SMEM] + [VMEM] * 6,
        out_specs=(VMEM,) * 4,
        scratch_shapes=[
            pltpu.VMEM((16, 8, 48, 128), F32),
            pltpu.VMEM((2 * 32 * 64, 128), F32),
        ],
        name="correct",
        cost_estimate=pl.CostEstimate(flops=4000000, bytes_accessed=3000000, transcendentals=0),
        compiler_params=pltpu.CompilerParams(vmem_limit_bytes=16 << 20),
    )(h, frames, up, dn, gain, couple, mask)


def correlate_kernel(h_ref, offo_ref, offr_ref, bins_ref, *refs):
    blocks, (out_ref, later, sums, table, off) = refs[:12], refs[12:]
    h = h_ref[0]
    for k in range(16):
        off[16 * h + k] = offo_ref[k]
        off[16 - 16 * h + k] = offr_ref[k]
    for b, first in enumerate((16 * h, 16 - 16 * h, 32 + 16 * h, 48 - 16 * h)):
        at = pl.multiple_of(4 * first, 64)
        for ref, row0, count in zip(blocks[3 * b : 3 * b + 3], (0, 24, 32), (24, 8, 24)):

            @pl.loop(0, count)
            def _(r, ref=ref, row0=row0, at=at):
                later[r + row0, pl.ds(at, 64), :] = ref[r].astype(F32)

    bin_id = lax.broadcasted_iota(jnp.int32, (32, 128), 0)

    @pl.loop(0, 4)
    def _(r8):
        for g in range(4):
            lane = pl.multiple_of(h * 512 + g * 128, 128)
            bins = bins_ref[pl.ds(pl.multiple_of(r8 * 8, 8), 8), pl.ds(lane, 128)]
            for i in range(8):
                at = pl.multiple_of(r8 * 1024 + i * 128, 128)
                hit = jnp.where(bins[i : i + 1] == bin_id, 1.0, 0.0)
                table[32 * g : 32 * g + 32, pl.ds(at, 128)] = hit.astype(BF16)

    low = lax.broadcasted_iota(jnp.int32, (8, 128), 0) < 4

    def one_row(r, carry):
        acc = [jnp.zeros((8, 128), F32) for _ in range(16)]
        for k in range(16):
            pair = later[r, 8 * k : 8 * k + 8, :]
            swap = pltpu.roll(pair, 4, 0)
            for odd in range(2):
                t = 2 * k + odd
                now = jnp.where(low, swap, pair) if odd else jnp.where(low, pair, swap)
                row = r + off[t]
                for j in range(16):
                    at = 4 * (t + 1 + 2 * j)
                    acc[j] = acc[j] + now * later[row, at : at + 8, :]
        at = pl.multiple_of(r * 128, 128)
        for j in range(8):
            two = jnp.concatenate([acc[2 * j], acc[2 * j + 1]], 0)
            high = two.astype(BF16)
            sums[16 * j : 16 * j + 16, pl.ds(at, 128)] = high
            rest = (two - high.astype(F32)).astype(BF16)
            sums[128 + 16 * j : 144 + 16 * j, pl.ds(at, 128)] = rest
        return carry

    lax.fori_loop(0, 32, one_row, 0)
    nt = (((1,), (1,)), ((), ()))
    both = lax.dot_general(sums[...], table[...], nt, preferred_element_type=F32)
    both = both[:128] + both[128:]
    row = lax.broadcasted_iota(jnp.int32, (128, 128), 0)
    col = lax.broadcasted_iota(jnp.int32, (128, 128), 1)
    both = jnp.where((row & 3) == (col >> 5), both, 0.0)
    q = lax.broadcasted_iota(jnp.int32, (32, 128), 0)
    lane = lax.broadcasted_iota(jnp.int32, (32, 128), 1)
    pick_q = jnp.where((lane & 31) == q, 1.0, 0.0)
    per_q = lax.dot_general(
        pick_q, both, nt, precision=lax.Precision.HIGHEST, preferred_element_type=F32
    )
    z = lax.broadcasted_iota(jnp.int32, (16, 128), 0)
    lane = lax.broadcasted_iota(jnp.int32, (16, 128), 1)
    for side in range(2):
        pick_l = jnp.where((lane >> 2) == 2 * z + side, 1.0, 0.0)
        part = lax.dot_general(
            per_q, pick_l, nt, precision=lax.Precision.HIGHEST, preferred_element_type=F32
        )
        for f in range(16):
            out_ref[2 * f + side] = part[2 * f : 2 * f + 2, :]


def correlate(h, off_own, off_other, bins, *blocks):
    return pl.pallas_call(
        correlate_kernel,
        out_shape=jax.ShapeDtypeStruct((32, 2, 16), F32),
        in_specs=[SMEM] * 3 + [VMEM] * 13,
        out_specs=VMEM,
        scratch_shapes=[
            pltpu.VMEM((56, 256, 128), F32),
            pltpu.VMEM((256, 4096), BF16),
            pltpu.VMEM((128, 4096), BF16),
            pltpu.SMEM((32,), jnp.int32),
        ],
        name="correlate",
        cost_estimate=pl.CostEstimate(flops=34000000, bytes_accessed=8000000, transcendentals=0),
        compiler_params=pltpu.CompilerParams(vmem_limit_bytes=24 << 20),
    )(h, off_own, off_other, bins, *blocks)


def per_device(frames, pixel_gain, couple, bin_index, pixel_mask, offsets):
    flow_count, time_count = lax.axis_size("flow"), lax.axis_size("tm")
    down = [(i, i + 1) for i in range(flow_count - 1)]
    up = [(i + 1, i) for i in range(flow_count - 1)]
    pair = [(i, i ^ 1) for i in range(time_count)]
    back = [(i + 2, i) for i in range(time_count - 2)]
    h = (lax.axis_index("tm") % 2).astype(jnp.int32).reshape(1)

    above = lax.ppermute(frames[:, 31, :], "flow", down)
    below = lax.ppermute(frames[:, 0, :], "flow", up)
    o24, o8, t24, t8 = correct(h, frames, above, below, pixel_gain, couple, pixel_mask)
    r24 = lax.ppermute(t24, "tm", pair)
    zo24 = lax.ppermute(o24, "tm", back)
    o_halo = lax.ppermute(o24, "flow", up)
    r8 = lax.ppermute(t8, "tm", pair)
    zo8 = lax.ppermute(o8, "tm", back)
    off_other = lax.ppermute(offsets, "tm", pair)
    r_halo = lax.ppermute(r24, "flow", up)
    zr24 = lax.ppermute(r24, "tm", back)
    zr8 = lax.ppermute(r8, "tm", back)
    zo_halo = lax.ppermute(zo24, "flow", up)
    zr_halo = lax.ppermute(zr24, "flow", up)
    part = correlate(
        h, offsets, off_other, bin_index,
        o24, o8, o_halo, r24, r8, r_halo, zo24, zo8, zo_halo, zr24, zr8, zr_halo,
    )
    both = ("flow", "tm")
    planes = [
        [f * time_count + 2 * z + s for f in range(flow_count) for s in range(2)]
        for z in range(time_count // 2)
    ]
    lines = [
        [f * time_count + 2 * z + s for z in range(time_count // 2)]
        for f in range(flow_count)
        for s in range(2)
    ]
    part = lax.all_to_all(part, both, 0, 0, axis_index_groups=planes).sum(0)
    part = lax.all_to_all(part.T.reshape(16, 1, 2), both, 0, 0, axis_index_groups=lines).sum(0)
    lag = (lax.axis_index("tm") + 1).astype(F32)
    normaliser = jnp.sqrt((16 * time_count - lag) * (32 * flow_count * 1024 / Q))
    return part.reshape(2, 1) / normaliser


def solution(mesh):
    in_specs = (
        P("tm", "flow", None),
        P("flow", None),
        P("flow", None),
        P("flow", None),
        P("flow", None),
        P("tm"),
    )
    return jax.shard_map(
        per_device, mesh=mesh, in_specs=in_specs, out_specs=P("flow", "tm"), check_vma=False
    )
```

time: 288 us -> 116 us (0.40)
  blocking collectives: 112 us -> 16.4 us
  other arithmetic: 45.8 us -> 0.6 us
  waiting for transfers between devices: 75.5 us -> 30.9 us
  starting transfers between devices: 14.7 us -> 51.6 us
  loops' own time: 30.2 us -> 0 us
  Pallas kernels: 0 us -> 12.1 us
  local copies, waits for them, and re-layouts: 7.2 us -> 3.14 us
    psum x1 -> x0, blocking collectives: 112 us -> none  [per_device(): total_sums = lax.psum(partial_sums, ('flow', 'tm'))]
    ppermute x5 -> x13, waiting for transfers between devices: 75.5 us -> 19.7 us  [the longest x1 8.73 us: per_device(): r24 = lax.ppermute(t24, 'tm', pair)]
    add x2 -> x0, other arithmetic: 31.6 us -> none  [add_group(): running = running + current[None] * window.astype(jnp.float32)]
    another operation x1 -> x0, loops' own time: 30.2 us -> none  [lagged_products(): lax.fori_loop(0, frame_count // 8, add_group, jnp.zeros((LAGS, lead_rows,...]
    ppermute x5 -> x13, starting transfers between devices: 14.7 us -> 35.2 us  [the longest x1 5.54 us: per_device(): below = lax.ppermute(frames[:, 0, :], 'flow', up)]
    all_to_all x0 -> x1, blocking collectives: none -> 16.4 us  [per_device(): part = lax.all_to_all(part, both, 0, 0, axis_index_groups=planes).sum(0)]
    all_to_all x0 -> x1, starting transfers between devices: none -> 16.3 us  [per_device(): lax.all_to_all(part.T.reshape(16, 1, 2), both, 0, 0, axis_index_groups=li...]
    pallas_call x0 -> x2, Pallas kernels: none -> 12.1 us  [the longest x1 9.39 us: correlate(): pl.pallas_call(correlate_kernel, out_shape=jax.ShapeDtypeStruct((32, 2, 1...]
  transfers between devices with their start and end apart: 5 -> 14, of which waited for: 3 -> 5; matrix products, arithmetic and copies ran while one was open for 0% -> 0% of each run, Pallas kernels for 0% -> 0%
where the time goes in v1:
time: 116 us; the launch traced here: 115 us
  starting transfers between devices  51.6 us (44%)
  waiting for transfers between devices  30.9 us (27%)
  blocking collectives  16.4 us (14%)
  Pallas kernels  12.1 us (10%)
  local copies, waits for them, and re-layouts  3.14 us (3%)
    all_to_all x1, blocking collectives, per_device(): part = lax.all_to_all(part, both, 0, 0, axis_index_groups=planes).sum(0)  16.4 us
    all_to_all x1, starting transfers between devices, per_device(): lax.all_to_all(part.T.reshape(16, 1, 2), both, 0, 0, axis_index_groups=li...  16.3 us
    all_to_all x1, waiting for transfers between devices, per_device(): lax.all_to_all(part.T.reshape(16, 1, 2), both, 0, 0, axis_index_groups=li...  11.2 us
    pallas_call x1, Pallas kernels, correlate(): pl.pallas_call(correlate_kernel, out_shape=jax.ShapeDtypeStruct((32, 2, 1...  9.39 us
    ppermute x1, waiting for transfers between devices, per_device(): r24 = lax.ppermute(t24, 'tm', pair)  8.73 us
    ppermute x1, starting transfers between devices, per_device(): below = lax.ppermute(frames[:, 0, :], 'flow', up)  5.54 us
    ppermute x1, waiting for transfers between devices, per_device(): zo8 = lax.ppermute(o8, 'tm', back)  5.32 us
    ppermute x1, waiting for transfers between devices, per_device(): zr8 = lax.ppermute(r8, 'tm', back)  4.86 us
  transfers between devices with their start and end apart: 14, of which 5 were waited for; matrix products, arithmetic and copies ran while one was open for 0% of the time, Pallas kernels for 0%

profile of v1, /device:TPU:1, one launch (start us, length us, event | category | flops | bytes accessed | tf_op | source)
XLA Modules:
  0.0 115.0 jit_solution(13588284186058181131)
XLA Ops:
  0.0 0.0 copy-start.3
  0.0 0.0 copy-start.4
  0.0 1.2 %fusion = (bf16[16,1,1024]{2,1,0:T(2,128)(2,1)S(1)}, bf16[16,1,1024]{2,1,0:T(2,128)(2,1)S(1)}) fusion(bf16[16,32,1024]{2,1,0:T(8,128)(2,1)} %f_ref.1), kind=kLoop, calls=%fused_computation.3 | loop fusion | bytes 131072 | tf_op jit(solution)/shard_map/slice | solution.py:181
  1.2 0.0 copy-start.2
  1.2 4.6 %collective-permute-start.1 = (bf16[16,1024]{1,0:T(8,128)(2,1)S(1)}, bf16[16,1024]{1,0:T(8,128)(2,1)S(1)}, u32[]{:S(2)}, u32[]{:S(2)}) collective-permute-start(bf16[16,1024]{1,0:T(8,128)(2,1)S(1)} %bitcast.12), channel_id=1, source_target_pairs={{0,32},{32,64},{64,96},{96,128},{128,160},{160,192},{192,224},{224... | collective-permute-start | bytes 98312 | tf_op jit(solution)/shard_map/ppermute | solution.py:180
  5.9 5.5 %collective-permute-start.2 = (bf16[16,1024]{1,0:T(8,128)(2,1)S(1)}, bf16[16,1024]{1,0:T(8,128)(2,1)S(1)}, u32[]{:S(2)}, u32[]{:S(2)}) collective-permute-start(bf16[16,1024]{1,0:T(8,128)(2,1)S(1)} %bitcast.13), channel_id=1, source_target_pairs={{32,0},{64,32},{96,64},{128,96},{160,128},{192,160},{224,192},{256... | collective-permute-start | bytes 98312 | tf_op jit(solution)/shard_map/ppermute | solution.py:181
  11.4 0.0 collective-permute-done.1.up_ref
  11.4 0.8 collective-permute-done.2.dn_ref
  12.3 0.0 copy-done.3
  12.3 0.0 copy-done.4
  12.3 0.0 copy-done.2
  12.3 0.0 copy-start
  12.3 1.2 %copy-done = bf16[16,32,1024]{2,1,0:T(8,128)(2,1)S(1)} copy-done((bf16[16,32,1024]{2,1,0:T(8,128)(2,1)S(1)}, bf16[16,32,1024]{2,1,0:T(8,128)(2,1)}, u32[]{:S(2)}) %copy-start) | copy-done | bytes 1048600
  13.5 0.0 copy-start.1
  13.5 2.8 %correct.1 = (bf16[24,64,128]{2,1,0:T(8,128)(2,1)S(1)}, bf16[8,64,128]{2,1,0:T(8,128)(2,1)S(1)}, bf16[24,64,128]{2,1,0:T(8,128)(2,1)S(1)}, bf16[8,64,128]{2,1,0:T(8,128)(2,1)S(1)}) custom-call(s32[1]{0:T(128)} %bitcast.h_ref, bf16[16,32,1024]{2,1,0:T(8,128)(2,1)S(1)} %copy-done, bf16[16,1024]{1,0:T(8,128)(2,1)S(1)} %collective-permute-done.1.up_ref, ...), custom_call_target="tpu_custom_call" | custom-call | flops 4000000 | bytes 3000000 | tf_op jit(solution)/shard_map/correct/pallas_call | solution.py:66
  16.3 3.7 %collective-permute-start.4 = (bf16[24,64,128]{2,1,0:T(8,128)(2,1)S(1)}, bf16[24,64,128]{2,1,0:T(8,128)(2,1)S(1)}, u32[]{:S(2)}, u32[]{:S(2)}) collective-permute-start(bf16[24,64,128]{2,1,0:T(8,128)(2,1)S(1)} %get-tuple-element.11), channel_id=1, source_target_pairs={{0,1},{1,0},{2,3},{3,2},{4,5},{5,4},{6,7},{7,6},{8,9},{9,8},{10,11... | collective-permute-start | bytes 1179656 | tf_op jit(solution)/shard_map/ppermute | solution.py:183
  20.0 0.0 copy-start.5
  20.0 1.3 %collective-permute-start.7 = (bf16[24,64,128]{2,1,0:T(8,128)(2,1)S(1)}, bf16[24,64,128]{2,1,0:T(8,128)(2,1)S(1)}, u32[]{:S(2)}, u32[]{:S(2)}) collective-permute-start(bf16[24,64,128]{2,1,0:T(8,128)(2,1)S(1)} %get-tuple-element.9.refs_0_), channel_id=1, source_target_pairs={{2,0},{3,1},{4,2},{5,3},{6,4},{7,5},{8,6},{9,7},{10,8},{11,9},{12,... | collective-permute-start | bytes 1179656 | tf_op jit(solution)/shard_map/ppermute | solution.py:184
  21.3 8.7 %collective-permute-done.4.refs_3_ = bf16[24,64,128]{2,1,0:T(8,128)(2,1)S(1)} collective-permute-done((bf16[24,64,128]{2,1,0:T(8,128)(2,1)S(1)}, bf16[24,64,128]{2,1,0:T(8,128)(2,1)S(1)}, u32[]{:S(2)}, u32[]{:S(2)}) %collective-permute-start.4) | collective-permute-done | bytes 393248 | tf_op jit(solution)/shard_map/ppermute | solution.py:183
  30.0 1.3 %collective-permute-start.10 = (bf16[24,64,128]{2,1,0:T(8,128)(2,1)S(1)}, bf16[24,64,128]{2,1,0:T(8,128)(2,1)S(1)}, u32[]{:S(2)}, u32[]{:S(2)}) collective-permute-start(bf16[24,64,128]{2,1,0:T(8,128)(2,1)S(1)} %collective-permute-done.4.refs_3_), channel_id=1, source_target_pairs={{2,0},{3,1},{4,2},{5,3},{6,4},{7,5},{8,6},{9,7},{10,8},{11,9},{12,... | collective-permute-start | bytes 1179656 | tf_op jit(solution)/shard_map/ppermute | solution.py:190
  31.3 3.0 %collective-permute-start.5 = (bf16[8,64,128]{2,1,0:T(8,128)(2,1)S(1)}, bf16[8,64,128]{2,1,0:T(8,128)(2,1)S(1)}, u32[]{:S(2)}, u32[]{:S(2)}) collective-permute-start(bf16[8,64,128]{2,1,0:T(8,128)(2,1)S(1)} %get-tuple-element.12), channel_id=1, source_target_pairs={{0,1},{1,0},{2,3},{3,2},{4,5},{5,4},{6,7},{7,6},{8,9},{9,8},{10,11... | collective-permute-start | bytes 393224 | tf_op jit(solution)/shard_map/ppermute | solution.py:186
  34.3 0.0 copy-done.5
  34.3 3.8 %collective-permute-start = (s32[16]{0:T(128)S(1)}, s32[16]{0:T(128)S(1)}, u32[]{:S(2)}, u32[]{:S(2)}) collective-permute-start(s32[16]{0:T(128)S(1)} %copy-done.5), channel_id=1, source_target_pairs={{0,1},{1,0},{2,3},{3,2},{4,5},{5,4},{6,7},{7,6},{8,9},{9,8},{10,11... | collective-permute-start | bytes 200 | tf_op jit(solution)/shard_map/ppermute | solution.py:188
  38.1 3.7 %collective-permute-start.3 = (bf16[24,64,128]{2,1,0:T(8,128)(2,1)S(1)}, bf16[24,64,128]{2,1,0:T(8,128)(2,1)S(1)}, u32[]{:S(2)}, u32[]{:S(2)}) collective-permute-start(bf16[24,64,128]{2,1,0:T(8,128)(2,1)S(1)} %get-tuple-element.9.refs_0_), channel_id=1, source_target_pairs={{32,0},{64,32},{96,64},{128,96},{160,128},{192,160},{224,192},{256... | collective-permute-start | bytes 1179656 | tf_op jit(solution)/shard_map/ppermute | solution.py:185
  41.8 0.0 collective-permute-done.offr_ref
  41.8 1.9 %collective-permute-start.6 = (bf16[24,64,128]{2,1,0:T(8,128)(2,1)S(1)}, bf16[24,64,128]{2,1,0:T(8,128)(2,1)S(1)}, u32[]{:S(2)}, u32[]{:S(2)}) collective-permute-start(bf16[24,64,128]{2,1,0:T(8,128)(2,1)S(1)} %collective-permute-done.4.refs_3_), channel_id=1, source_target_pairs={{32,0},{64,32},{96,64},{128,96},{160,128},{192,160},{224,192},{256... | collective-permute-start | bytes 1179656 | tf_op jit(solution)/shard_map/ppermute | solution.py:189
  43.7 0.0 collective-permute-done.7.refs_6_
  43.7 1.9 %collective-permute-start.9 = (bf16[24,64,128]{2,1,0:T(8,128)(2,1)S(1)}, bf16[24,64,128]{2,1,0:T(8,128)(2,1)S(1)}, u32[]{:S(2)}, u32[]{:S(2)}) collective-permute-start(bf16[24,64,128]{2,1,0:T(8,128)(2,1)S(1)} %collective-permute-done.7.refs_6_), channel_id=1, source_target_pairs={{32,0},{64,32},{96,64},{128,96},{160,128},{192,160},{224,192},{256... | collective-permute-start | bytes 1179656 | tf_op jit(solution)/shard_map/ppermute | solution.py:192
  45.7 0.0 collective-permute-done.10.refs_9_
  45.7 1.9 %collective-permute-start.12 = (bf16[24,64,128]{2,1,0:T(8,128)(2,1)S(1)}, bf16[24,64,128]{2,1,0:T(8,128)(2,1)S(1)}, u32[]{:S(2)}, u32[]{:S(2)}) collective-permute-start(bf16[24,64,128]{2,1,0:T(8,128)(2,1)S(1)} %collective-permute-done.10.refs_9_), channel_id=1, source_target_pairs={{32,0},{64,32},{96,64},{128,96},{160,128},{192,160},{224,192},{256... | collective-permute-start | bytes 1179656 | tf_op jit(solution)/shard_map/ppermute | solution.py:193
  47.6 0.0 collective-permute-done.5.refs_4_
  47.6 1.3 %collective-permute-start.8 = (bf16[8,64,128]{2,1,0:T(8,128)(2,1)S(1)}, bf16[8,64,128]{2,1,0:T(8,128)(2,1)S(1)}, u32[]{:S(2)}, u32[]{:S(2)}) collective-permute-start(bf16[8,64,128]{2,1,0:T(8,128)(2,1)S(1)} %get-tuple-element.10.refs_1_), channel_id=1, source_target_pairs={{2,0},{3,1},{4,2},{5,3},{6,4},{7,5},{8,6},{9,7},{10,8},{11,9},{12,... | collective-permute-start | bytes 393224 | tf_op jit(solution)/shard_map/ppermute | solution.py:187
  48.9 5.3 %collective-permute-done.8.refs_7_ = bf16[8,64,128]{2,1,0:T(8,128)(2,1)S(1)} collective-permute-done((bf16[8,64,128]{2,1,0:T(8,128)(2,1)S(1)}, bf16[8,64,128]{2,1,0:T(8,128)(2,1)S(1)}, u32[]{:S(2)}, u32[]{:S(2)}) %collective-permute-start.8) | collective-permute-done | bytes 131104 | tf_op jit(solution)/shard_map/ppermute | solution.py:187
  54.2 1.3 %collective-permute-start.11 = (bf16[8,64,128]{2,1,0:T(8,128)(2,1)S(1)}, bf16[8,64,128]{2,1,0:T(8,128)(2,1)S(1)}, u32[]{:S(2)}, u32[]{:S(2)}) collective-permute-start(bf16[8,64,128]{2,1,0:T(8,128)(2,1)S(1)} %collective-permute-done.5.refs_4_), channel_id=1, source_target_pairs={{2,0},{3,1},{4,2},{5,3},{6,4},{7,5},{8,6},{9,7},{10,8},{11,9},{12,... | collective-permute-start | bytes 393224 | tf_op jit(solution)/shard_map/ppermute | solution.py:191
  55.5 4.9 %collective-permute-done.11.refs_10_ = bf16[8,64,128]{2,1,0:T(8,128)(2,1)S(1)} collective-permute-done((bf16[8,64,128]{2,1,0:T(8,128)(2,1)S(1)}, bf16[8,64,128]{2,1,0:T(8,128)(2,1)S(1)}, u32[]{:S(2)}, u32[]{:S(2)}) %collective-permute-start.11) | collective-permute-done | bytes 131104 | tf_op jit(solution)/shard_map/ppermute | solution.py:191
  60.4 0.0 collective-permute-done.3.refs_2_
  60.4 0.0 collective-permute-done.6.refs_5_
  60.4 0.0 collective-permute-done.9.refs_8_
  60.4 0.0 collective-permute-done.12.refs_11_
  60.4 0.0 copy-done.1
  60.4 9.4 %correlate.1 = f32[32,2,16]{2,1,0:T(2,128)S(1)} custom-call(s32[1]{0:T(128)} %bitcast.h_ref, s32[16]{0:T(128)S(1)} %copy-done.5, s32[16]{0:T(128)S(1)} %collective-permute-done.offr_ref, s32[32,1024]{1,0:T(8,128)S(1)} %copy-done.1, bf16[24,64,128]{2,1,0:T(8,128)(2,1)S(1)} %get-tuple-element.9.refs_0_, bf16[8,64,128]{2,1,0:T(8,128)(2,1)S(1)} %get-tuple-element.10.refs_1_, ...), custom_call_target="tpu_custom_call" | custom-call | flops 34000000 | bytes 8000000 | tf_op jit(solution)/shard_map/correlate/pallas_call | solution.py:155
  69.8 16.4 %all_to_all.10 = f32[32,2,16]{2,1,0:T(2,128)S(1)} all-to-all(f32[32,2,16]{2,1,0:T(2,128)S(1)} %correlate.1), channel_id=1, replica_groups={{0,1,32,33,64,65,96,97,128,129,160,161,192,193,224,225,256,257,288,289,..., dimensions={0} | all-to-all | bytes 8192 | tf_op jit(solution)/shard_map/all_to_all | solution.py:208
  86.2 0.7 copy.11
  86.9 16.3 %all-to-all-start.1 = ((f32[16,1,2]{2,1,0:T(1,128)}), f32[16,1,2]{2,1,0:T(1,128)S(1)}, u32[]{:S(2)}, u32[]{:S(2)}) async-start(f32[16,1,2]{2,1,0:T(1,128)} %copy.11), calls=%async_computation.1 | async-start | bytes 16384 | tf_op jit(solution)/shard_map/all_to_all | solution.py:209
  103.3 11.2 %all-to-all-done.1 = f32[16,1,2]{2,1,0:T(1,128)S(1)} async-done(((f32[16,1,2]{2,1,0:T(1,128)}), f32[16,1,2]{2,1,0:T(1,128)S(1)}, u32[]{:S(2)}, u32[]{:S(2)}) %all-to-all-start.1) | async-done | bytes 160 | tf_op jit(solution)/shard_map/all_to_all | solution.py:209
  114.5 0.5 divide_bitcast_fusion
  (4 shorter events, 0.1 us)
Async XLA Ops:
  0.0 12.3 %copy-start.3 = (f32[32,1024]{1,0:T(8,128)S(1)}, f32[32,1024]{1,0:T(8,128)}, u32[]{:S(2)}) copy-start(f32[32,1024]{1,0:T(8,128)} %couple_ref.1) | copy-start | bytes 393220
  0.0 12.3 %copy-start.4 = (s32[32,1024]{1,0:T(8,128)S(1)}, s32[32,1024]{1,0:T(8,128)}, u32[]{:S(2)}) copy-start(s32[32,1024]{1,0:T(8,128)} %mask_ref.1) | copy-start | bytes 393220
  1.2 11.1 %copy-start.2 = (f32[32,1024]{1,0:T(8,128)S(1)}, f32[32,1024]{1,0:T(8,128)}, u32[]{:S(2)}) copy-start(f32[32,1024]{1,0:T(8,128)} %gain_ref.1) | copy-start | bytes 393220
  1.2 10.2 %collective-permute-start.1 = (bf16[16,1024]{1,0:T(8,128)(2,1)S(1)}, bf16[16,1024]{1,0:T(8,128)(2,1)S(1)}, u32[]{:S(2)}, u32[]{:S(2)}) collective-permute-start(bf16[16,1024]{1,0:T(8,128)(2,1)S(1)} %bitcast.12), channel_id=1, source_target_pairs={{0,32},{32,64},{64,96},{96,128},{128,160},{160,192},{192,224},{224... | collective-permute-start | bytes 98312 | tf_op jit(solution)/shard_map/ppermute | solution.py:180
  5.9 6.4 %collective-permute-start.2 = (bf16[16,1024]{1,0:T(8,128)(2,1)S(1)}, bf16[16,1024]{1,0:T(8,128)(2,1)S(1)}, u32[]{:S(2)}, u32[]{:S(2)}) collective-permute-start(bf16[16,1024]{1,0:T(8,128)(2,1)S(1)} %bitcast.13), channel_id=1, source_target_pairs={{32,0},{64,32},{96,64},{128,96},{160,128},{192,160},{224,192},{256... | collective-permute-start | bytes 98312 | tf_op jit(solution)/shard_map/ppermute | solution.py:181
  12.3 1.2 %copy-start = (bf16[16,32,1024]{2,1,0:T(8,128)(2,1)S(1)}, bf16[16,32,1024]{2,1,0:T(8,128)(2,1)}, u32[]{:S(2)}) copy-start(bf16[16,32,1024]{2,1,0:T(8,128)(2,1)} %f_ref.1) | copy-start | bytes 3145732
  13.5 46.9 %copy-start.1 = (s32[32,1024]{1,0:T(8,128)S(1)}, s32[32,1024]{1,0:T(8,128)}, u32[]{:S(2)}) copy-start(s32[32,1024]{1,0:T(8,128)} %bins_ref.1) | copy-start | bytes 393220
  16.3 13.7 %collective-permute-start.4 = (bf16[24,64,128]{2,1,0:T(8,128)(2,1)S(1)}, bf16[24,64,128]{2,1,0:T(8,128)(2,1)S(1)}, u32[]{:S(2)}, u32[]{:S(2)}) collective-permute-start(bf16[24,64,128]{2,1,0:T(8,128)(2,1)S(1)} %get-tuple-element.11), channel_id=1, source_target_pairs={{0,1},{1,0},{2,3},{3,2},{4,5},{5,4},{6,7},{7,6},{8,9},{9,8},{10,11... | collective-permute-start | bytes 1179656 | tf_op jit(solution)/shard_map/ppermute | solution.py:183
  20.0 14.3 %copy-start.5 = (s32[16]{0:T(128)S(1)}, s32[16]{0:T(128)}, u32[]{:S(2)}) copy-start(s32[16]{0:T(128)} %offo_ref.1) | copy-start | bytes 196
  20.0 23.8 %collective-permute-start.7 = (bf16[24,64,128]{2,1,0:T(8,128)(2,1)S(1)}, bf16[24,64,128]{2,1,0:T(8,128)(2,1)S(1)}, u32[]{:S(2)}, u32[]{:S(2)}) collective-permute-start(bf16[24,64,128]{2,1,0:T(8,128)(2,1)S(1)} %get-tuple-element.9.refs_0_), channel_id=1, source_target_pairs={{2,0},{3,1},{4,2},{5,3},{6,4},{7,5},{8,6},{9,7},{10,8},{11,9},{12,... | collective-permute-start | bytes 1179656 | tf_op jit(solution)/shard_map/ppermute | solution.py:184
  30.0 15.7 %collective-permute-start.10 = (bf16[24,64,128]{2,1,0:T(8,128)(2,1)S(1)}, bf16[24,64,128]{2,1,0:T(8,128)(2,1)S(1)}, u32[]{:S(2)}, u32[]{:S(2)}) collective-permute-start(bf16[24,64,128]{2,1,0:T(8,128)(2,1)S(1)} %collective-permute-done.4.refs_3_), channel_id=1, source_target_pairs={{2,0},{3,1},{4,2},{5,3},{6,4},{7,5},{8,6},{9,7},{10,8},{11,9},{12,... | collective-permute-start | bytes 1179656 | tf_op jit(solution)/shard_map/ppermute | solution.py:190
  31.3 16.3 %collective-permute-start.5 = (bf16[8,64,128]{2,1,0:T(8,128)(2,1)S(1)}, bf16[8,64,128]{2,1,0:T(8,128)(2,1)S(1)}, u32[]{:S(2)}, u32[]{:S(2)}) collective-permute-start(bf16[8,64,128]{2,1,0:T(8,128)(2,1)S(1)} %get-tuple-element.12), channel_id=1, source_target_pairs={{0,1},{1,0},{2,3},{3,2},{4,5},{5,4},{6,7},{7,6},{8,9},{9,8},{10,11... | collective-permute-start | bytes 393224 | tf_op jit(solution)/shard_map/ppermute | solution.py:186
  34.3 7.5 %collective-permute-start = (s32[16]{0:T(128)S(1)}, s32[16]{0:T(128)S(1)}, u32[]{:S(2)}, u32[]{:S(2)}) collective-permute-start(s32[16]{0:T(128)S(1)} %copy-done.5), channel_id=1, source_target_pairs={{0,1},{1,0},{2,3},{3,2},{4,5},{5,4},{6,7},{7,6},{8,9},{9,8},{10,11... | collective-permute-start | bytes 200 | tf_op jit(solution)/shard_map/ppermute | solution.py:188
  38.1 22.3 %collective-permute-start.3 = (bf16[24,64,128]{2,1,0:T(8,128)(2,1)S(1)}, bf16[24,64,128]{2,1,0:T(8,128)(2,1)S(1)}, u32[]{:S(2)}, u32[]{:S(2)}) collective-permute-start(bf16[24,64,128]{2,1,0:T(8,128)(2,1)S(1)} %get-tuple-element.9.refs_0_), channel_id=1, source_target_pairs={{32,0},{64,32},{96,64},{128,96},{160,128},{192,160},{224,192},{256... | collective-permute-start | bytes 1179656 | tf_op jit(solution)/shard_map/ppermute | solution.py:185
  41.8 18.6 %collective-permute-start.6 = (bf16[24,64,128]{2,1,0:T(8,128)(2,1)S(1)}, bf16[24,64,128]{2,1,0:T(8,128)(2,1)S(1)}, u32[]{:S(2)}, u32[]{:S(2)}) collective-permute-start(bf16[24,64,128]{2,1,0:T(8,128)(2,1)S(1)} %collective-permute-done.4.refs_3_), channel_id=1, source_target_pairs={{32,0},{64,32},{96,64},{128,96},{160,128},{192,160},{224,192},{256... | collective-permute-start | bytes 1179656 | tf_op jit(solution)/shard_map/ppermute | solution.py:189
  43.7 16.7 %collective-permute-start.9 = (bf16[24,64,128]{2,1,0:T(8,128)(2,1)S(1)}, bf16[24,64,128]{2,1,0:T(8,128)(2,1)S(1)}, u32[]{:S(2)}, u32[]{:S(2)}) collective-permute-start(bf16[24,64,128]{2,1,0:T(8,128)(2,1)S(1)} %collective-permute-done.7.refs_6_), channel_id=1, source_target_pairs={{32,0},{64,32},{96,64},{128,96},{160,128},{192,160},{224,192},{256... | collective-permute-start | bytes 1179656 | tf_op jit(solution)/shard_map/ppermute | solution.py:192
  45.7 14.7 %collective-permute-start.12 = (bf16[24,64,128]{2,1,0:T(8,128)(2,1)S(1)}, bf16[24,64,128]{2,1,0:T(8,128)(2,1)S(1)}, u32[]{:S(2)}, u32[]{:S(2)}) collective-permute-start(bf16[24,64,128]{2,1,0:T(8,128)(2,1)S(1)} %collective-permute-done.10.refs_9_), channel_id=1, source_target_pairs={{32,0},{64,32},{96,64},{128,96},{160,128},{192,160},{224,192},{256... | collective-permute-start | bytes 1179656 | tf_op jit(solution)/shard_map/ppermute | solution.py:193
  47.6 6.6 %collective-permute-start.8 = (bf16[8,64,128]{2,1,0:T(8,128)(2,1)S(1)}, bf16[8,64,128]{2,1,0:T(8,128)(2,1)S(1)}, u32[]{:S(2)}, u32[]{:S(2)}) collective-permute-start(bf16[8,64,128]{2,1,0:T(8,128)(2,1)S(1)} %get-tuple-element.10.refs_1_), channel_id=1, source_target_pairs={{2,0},{3,1},{4,2},{5,3},{6,4},{7,5},{8,6},{9,7},{10,8},{11,9},{12,... | collective-permute-start | bytes 393224 | tf_op jit(solution)/shard_map/ppermute | solution.py:187
  54.2 6.1 %collective-permute-start.11 = (bf16[8,64,128]{2,1,0:T(8,128)(2,1)S(1)}, bf16[8,64,128]{2,1,0:T(8,128)(2,1)S(1)}, u32[]{:S(2)}, u32[]{:S(2)}) collective-permute-start(bf16[8,64,128]{2,1,0:T(8,128)(2,1)S(1)} %collective-permute-done.5.refs_4_), channel_id=1, source_target_pairs={{2,0},{3,1},{4,2},{5,3},{6,4},{7,5},{8,6},{9,7},{10,8},{11,9},{12,... | collective-permute-start | bytes 393224 | tf_op jit(solution)/shard_map/ppermute | solution.py:191
  86.9 27.6 %all-to-all-start.1 = ((f32[16,1,2]{2,1,0:T(1,128)}), f32[16,1,2]{2,1,0:T(1,128)S(1)}, u32[]{:S(2)}, u32[]{:S(2)}) async-start(f32[16,1,2]{2,1,0:T(1,128)} %copy.11), calls=%async_computation.1 | async-start | bytes 16384 | tf_op jit(solution)/shard_map/all_to_all | solution.py:209

commit v2 on v1

v2 whole, which is shorter than its diff:
```python
import jax
import jax.numpy as jnp
from jax import lax
from jax.experimental import pallas as pl
from jax.experimental.pallas import tpu as pltpu
from jax.sharding import PartitionSpec as P

LAGS = 32
OFF_MAX = 24
Q = 32
F32, BF16 = jnp.float32, jnp.bfloat16
VMEM = pl.BlockSpec(memory_space=pltpu.VMEM)
SMEM = pl.BlockSpec(memory_space=pltpu.SMEM)
NT = (((1,), (1,)), ((), ()))


def split_kernel(
    h_ref, f_ref, gain_ref, couple_ref, mask_ref, back, fwd, swap, up, down, coef, coef_up, work
):
    h = h_ref[0]

    @pl.loop(0, 16)
    def _(f):
        for j in range(8):
            cols = slice(128 * j, 128 * j + 128)
            start = (j // 4) * 2048 + (j % 4) + 4 * f
            for k in range(2):
                value = f_ref[f, 16 * k : 16 * k + 16, cols].astype(F32)
                work[pl.ds(start + 1024 * k, 8, stride=64), :] = value[:8]
                work[pl.ds(start + 1024 * k + 512, 8, stride=64), :] = value[8:]

    def row_of(half, r):
        return work[pl.ds(pl.multiple_of(half * 2048 + r * 64, 64), 64), :].astype(BF16)

    @pl.loop(0, 32)
    def _(r):
        back[r] = row_of(0, r)
        fwd[r] = row_of(1, r)
        swap[r] = row_of(1 - h, r)

    @pl.loop(0, 25)
    def _(r):
        up[r] = row_of(0, r)
        up[r + 25] = row_of(1, r)

    for half in range(2):
        down[half] = row_of(half, 31)
    for k in range(4):
        for j in range(8):
            rows, cols = slice(8 * k, 8 * k + 8), slice(128 * j, 128 * j + 128)
            good = mask_ref[rows, cols].astype(F32)
            at = pl.ds(32 * k + j % 4, 8, stride=4)
            for c, ref in enumerate((gain_ref, couple_ref)):
                value = ref[rows, cols] * good
                coef[c, j // 4, at, :] = value
                if k < 3:
                    coef_up[c, j // 4, at, :] = value


def split(h, frames, gain, couple, mask):
    block = lambda n: jax.ShapeDtypeStruct((n, 64, 128), BF16)
    return pl.pallas_call(
        split_kernel,
        out_shape=(
            block(32),
            block(32),
            block(32),
            block(50),
            block(2),
            jax.ShapeDtypeStruct((2, 2, 128, 128), F32),
            jax.ShapeDtypeStruct((2, 2, 96, 128), F32),
        ),
        in_specs=[SMEM] + [VMEM] * 4,
        out_specs=(VMEM,) * 7,
        scratch_shapes=[pltpu.VMEM((2 * 32 * 64, 128), F32)],
        name="split",
        cost_estimate=pl.CostEstimate(flops=1000000, bytes_accessed=3000000, transcendentals=0),
        compiler_params=pltpu.CompilerParams(vmem_limit_bytes=12 << 20),
    )(h, frames, gain, couple, mask)


def low_half():
    return lax.broadcasted_iota(jnp.int32, (8, 128), 0) < 4


def correct_rows(raw, coef, coef_up, half, count, put):
    low = low_half()

    def rows(k, source, at):
        pair = [source[c, half, pl.ds(pl.multiple_of(8 * at, 8), 8), :] for c in range(2)]
        swap = [pltpu.roll(v, 4, 0) for v in pair]
        line = [raw[2 * k + i].astype(F32) for i in range(4)]
        for odd in range(2):
            gain, couple = (
                jnp.where(low, s, v) if odd else jnp.where(low, v, s) for v, s in zip(pair, swap)
            )
            parts = []
            for i in range(8):
                at8 = slice(8 * i, 8 * i + 8)
                beside = line[odd][at8] + line[odd + 2][at8]
                parts.append(gain * line[odd + 1][at8] + couple * beside)
            put(2 * k + odd, jnp.concatenate(parts, 0).astype(BF16))

    @pl.loop(0, 16)
    def _(k):
        rows(k, coef, k)

    if count > 32:

        @pl.loop(16, count // 2)
        def _(k):
            rows(k, coef_up, k - 16)


def twice(pair, swap, odd, low):
    return jnp.where(low, swap, pair) if odd else jnp.where(low, pair, swap)


def own_kernel(
    h_ref, off_ref, bins_ref, half0, half1, above, below, coef, coef_up, fixed, acc_ref, table, raw, work
):
    h = h_ref[0]
    low = low_half()
    work[:, :, 64:72, :] = jnp.zeros((2, 56, 8, 128), F32)
    for half, main in enumerate((half0, half1)):
        raw[0] = above[half]

        @pl.loop(0, 32)
        def _(r, main=main):
            raw[r + 1] = main[r]

        @pl.loop(0, 25)
        def _(r, half=half):
            raw[r + 33] = below[25 * half + r]

        role = h if half == 0 else 1 - h

        def put(r, value, role=role):
            fixed[role, r] = value
            work[role, r, 0:64, :] = value.astype(F32)

        correct_rows(raw, coef, coef_up, half, 56, put)
    bin_id = lax.broadcasted_iota(jnp.int32, (32, 128), 0)
    for role in range(2):

        @pl.loop(0, 4)
        def _(r8, role=role):
            half = h if role == 0 else 1 - h
            for g in range(4):
                lane = pl.multiple_of(half * 512 + g * 128, 128)
                bins = bins_ref[pl.ds(pl.multiple_of(r8 * 8, 8), 8), pl.ds(lane, 128)]
                for i in range(8):
                    at = pl.multiple_of(role * 4096 + r8 * 1024 + i * 128, 128)
                    hit = jnp.where(bins[i : i + 1] == bin_id, 1.0, 0.0)
                    table[32 * g : 32 * g + 32, pl.ds(at, 128)] = hit.astype(BF16)

        @pl.loop(0, 32)
        def _(r, role=role):
            acc = [jnp.zeros((8, 128), F32) for _ in range(8)]
            for k in range(8):
                pair = work[role, r, 8 * k : 8 * k + 8, :]
                swap = pltpu.roll(pair, 4, 0)
                for odd in range(2):
                    t = 2 * k + odd
                    now = twice(pair, swap, odd, low)
                    row = r + off_ref[t]
                    for j in range((16 - t) // 2):
                        at = 4 * (t + 1 + 2 * j)
                        acc[j] = acc[j] + now * work[role, row, at : at + 8, :]
            for j in range(8):
                acc_ref[role, r, j] = acc[j]


def own_part(h, off, bins, half0, half1, above, below, coef, coef_up):
    return pl.pallas_call(
        own_kernel,
        out_shape=(
            jax.ShapeDtypeStruct((2, 56, 64, 128), BF16),
            jax.ShapeDtypeStruct((2, 32, 8, 8, 128), F32),
            jax.ShapeDtypeStruct((128, 8192), BF16),
        ),
        in_specs=[SMEM] * 2 + [VMEM] * 7,
        out_specs=(VMEM,) * 3,
        scratch_shapes=[pltpu.VMEM((58, 64, 128), BF16), pltpu.VMEM((2, 56, 72, 128), F32)],
        name="own",
        cost_estimate=pl.CostEstimate(flops=12000000, bytes_accessed=9000000, transcendentals=0),
        compiler_params=pltpu.CompilerParams(vmem_limit_bytes=20 << 20),
    )(h, off, bins, half0, half1, above, below, coef, coef_up)


def lag_kernel(
    h_ref, off_own, off_other, off_back, fixed, acc_ref, table, coef, coef_up,
    other, back, fwd, above, other_below, two_below, out_ref, raw, later, sums, off,
):
    h = h_ref[0]
    low = low_half()
    for k in range(16):
        off[48 * h + k] = off_own[k]
        off[16 + k] = off_other[k]
        off[48 - 48 * h + k] = off_back[k]
    at_own = [pl.multiple_of(128 * h, 64), pl.multiple_of(256 - 64 * h, 64)]
    at_back = pl.multiple_of(128 + 128 * h, 64)
    at_fwd = pl.multiple_of(192 - 192 * h, 64)
    later[:, 320:328, :] = jnp.zeros((56, 8, 128), F32)

    @pl.loop(0, 56)
    def _(r):
        for role in range(2):
            later[r, pl.ds(at_own[role], 64), :] = fixed[role, r].astype(F32)

    @pl.loop(32, 56)
    def _(r):
        later[r, pl.ds(at_fwd, 64), :] = jnp.zeros((64, 128), F32)

    for which, (main, half, count, at) in enumerate(
        ((other, h, 56, 64), (back, 0, 56, at_back), (fwd, 1, 32, at_fwd))
    ):
        raw[0] = above[which]

        @pl.loop(0, 32)
        def _(r, main=main):
            raw[r + 1] = main[r]

        if which == 2:
            raw[33] = two_below[25]
        else:
            below = two_below if which else other_below

            @pl.loop(0, 25)
            def _(r, below=below):
                raw[r + 33] = below[r]

        def put(r, value, at=at):
            later[r, pl.ds(at, 64), :] = value.astype(F32)

        correct_rows(raw, coef, coef_up, half, count, put)

    zero = jnp.zeros((8, 128), F32)

    def store(acc, at):
        at = pl.multiple_of(at, 128)
        for j in range(8):
            two = jnp.concatenate([acc[2 * j], acc[2 * j + 1]], 0)
            high = two.astype(BF16)
            sums[16 * j : 16 * j + 16, pl.ds(at, 128)] = high
            rest = (two - high.astype(F32)).astype(BF16)
            sums[128 + 16 * j : 144 + 16 * j, pl.ds(at, 128)] = rest

    def add_from(acc, r, source, target, off_at, first_lag, last_lag):
        for k in range(8):
            pair = later[r, source + 8 * k : source + 8 * k + 8, :]
            swap = pltpu.roll(pair, 4, 0)
            for odd in range(2):
                i = 2 * k + odd
                now = twice(pair, swap, odd, low)
                row = r + off[off_at + i]
                first, last = first_lag - i, last_lag(i)
                for j in range((first - 1) // 2, (last - 1) // 2 + 1):
                    x = now
                    if 2 * j + 1 < first:
                        x = jnp.where(low, 0.0, x)
                    if 2 * j + 2 > last:
                        x = jnp.where(low, x, 0.0)
                    at = target + 4 * (2 * j + 1 - first)
                    acc[j] = acc[j] + x * later[row, at : at + 8, :]

    @pl.loop(0, 32)
    def _(r):
        acc = [acc_ref[0, r, j] for j in range(8)] + [zero] * 8
        add_from(acc, r, 0, 64, 0, 16, lambda i: 32)
        add_from(acc, r, 64, 128, 16, 16, lambda i: 31 - i)
        store(acc, r * 128)
        acc = [acc_ref[1, r, j] for j in range(8)] + [zero] * 8
        add_from(acc, r, 192, 256, 48, 32, lambda i: 32)
        store(acc, 4096 + r * 128)

    both = lax.dot_general(sums[...], table[...], NT, preferred_element_type=F32)
    both = both[:128] + both[128:]
    row = lax.broadcasted_iota(jnp.int32, (128, 128), 0)
    col = lax.broadcasted_iota(jnp.int32, (128, 128), 1)
    both = jnp.where((row & 3) == (col >> 5), both, 0.0)
    q = lax.broadcasted_iota(jnp.int32, (32, 128), 0)
    lane = lax.broadcasted_iota(jnp.int32, (32, 128), 1)
    pick_q = jnp.where((lane & 31) == q, 1.0, 0.0)
    per_q = lax.dot_general(
        pick_q, both, NT, precision=lax.Precision.HIGHEST, preferred_element_type=F32
    )
    z = lax.broadcasted_iota(jnp.int32, (16, 128), 0)
    lane = lax.broadcasted_iota(jnp.int32, (16, 128), 1)
    for side in range(2):
        pick_l = jnp.where((lane >> 2) == 2 * z + side, 1.0, 0.0)
        part = lax.dot_general(
            per_q, pick_l, NT, precision=lax.Precision.HIGHEST, preferred_element_type=F32
        )
        for f in range(16):
            out_ref[2 * f + side] = part[2 * f : 2 * f + 2, :]


def lag_part(h, offs, fixed, acc, table, coef, coef_up, blocks):
    return pl.pallas_call(
        lag_kernel,
        out_shape=jax.ShapeDtypeStruct((32, 2, 16), F32),
        in_specs=[SMEM] * 4 + [VMEM] * 11,
        out_specs=VMEM,
        scratch_shapes=[
            pltpu.VMEM((58, 64, 128), BF16),
            pltpu.VMEM((56, 328, 128), F32),
            pltpu.VMEM((256, 8192), BF16),
            pltpu.SMEM((64,), jnp.int32),
        ],
        name="lags",
        cost_estimate=pl.CostEstimate(flops=34000000, bytes_accessed=12000000, transcendentals=0),
        compiler_params=pltpu.CompilerParams(vmem_limit_bytes=24 << 20),
    )(h, *offs, fixed, acc, table, coef, coef_up, *blocks)


def per_device(frames, pixel_gain, couple, bin_index, pixel_mask, offsets):
    flow_count, time_count = lax.axis_size("flow"), lax.axis_size("tm")
    down = [(i, i + 1) for i in range(flow_count - 1)]
    up = [(i + 1, i) for i in range(flow_count - 1)]
    pair = [(i, i ^ 1) for i in range(time_count)]
    backward = [(i + 2, i) for i in range(time_count - 2)]
    forward = [(i, i + 2) for i in range(time_count - 2)]
    h = (lax.axis_index("tm") % 2).astype(jnp.int32).reshape(1)

    half0, half1, swap, own_up, own_down, coef, coef_up = split(
        h, frames, pixel_gain, couple, pixel_mask
    )
    other = lax.ppermute(swap, "tm", pair)
    back = lax.ppermute(half0, "tm", backward)
    fwd = lax.ppermute(half1, "tm", forward)
    own_below = lax.ppermute(own_up, "flow", up)
    own_above = lax.ppermute(own_down, "flow", down)
    coef_below = lax.ppermute(coef_up, "flow", up)
    off_other = lax.ppermute(offsets, "tm", pair)
    off_back = lax.ppermute(offsets, "tm", forward)
    other_below = lax.ppermute(other[:25], "flow", up)
    two_below = lax.ppermute(jnp.concatenate([back[:25], fwd[:1]], 0), "flow", up)
    above = lax.ppermute(jnp.stack([other[31], back[31], fwd[31]]), "flow", down)
    fixed, acc, table = own_part(
        h, offsets, bin_index, half0, half1, own_above, own_below, coef, coef_below
    )
    part = lag_part(
        h, (offsets, off_other, off_back), fixed, acc, table, coef, coef_below,
        (other, back, fwd, above, other_below, two_below),
    )
    both = ("flow", "tm")
    planes = [
        [f * time_count + 2 * z + s for f in range(flow_count) for s in range(2)]
        for z in range(time_count // 2)
    ]
    lines = [
        [f * time_count + 2 * z + s for z in range(time_count // 2)]
        for f in range(flow_count)
        for s in range(2)
    ]
    lag = (lax.axis_index("tm") + 1).astype(F32)
    normaliser = jnp.sqrt((16 * time_count - lag) * (32 * flow_count * 1024 / Q))
    part, normaliser = lax.optimization_barrier((part, normaliser))
    part = lax.all_to_all(part, both, 0, 0, axis_index_groups=planes).sum(0)
    part = lax.all_to_all(part.T.reshape(16, 1, 2), both, 0, 0, axis_index_groups=lines).sum(0)
    return part.reshape(2, 1) / normaliser


def solution(mesh):
    in_specs = (
        P("tm", "flow", None),
        P("flow", None),
        P("flow", None),
        P("flow", None),
        P("flow", None),
        P("tm"),
    )
    return jax.shard_map(
        per_device, mesh=mesh, in_specs=in_specs, out_specs=P("flow", "tm"), check_vma=False
    )
```

time: 116 us -> 131 us (1.13)
  blocking collectives: 16.4 us -> 56.3 us
  waiting for transfers between devices: 30.9 us -> 0.39 us
  Pallas kernels: 12.1 us -> 20.7 us
  starting transfers between devices: 51.6 us -> 43.1 us
  local copies, waits for them, and re-layouts: 3.14 us -> 7.92 us
  other arithmetic: 0.6 us -> 2.03 us
    all_to_all x0 -> x1, blocking collectives: none -> 25.6 us  [per_device(): lax.all_to_all(part.T.reshape(16, 1, 2), both, 0, 0, axis_index_groups=li...]
    ppermute x12 -> x10, waiting for transfers between devices: 19.7 us -> 0.38 us  [the longest x1 0.36 us: per_device(): own_above = lax.ppermute(own_down, 'flow', down)]
    all_to_all x1 -> x0, starting transfers between devices: 16.3 us -> none  [per_device(): lax.all_to_all(part.T.reshape(16, 1, 2), both, 0, 0, axis_index_groups=li...]
    all_to_all x1, blocking collectives: 16.4 us -> 30.7 us  [per_device(): part = lax.all_to_all(part, both, 0, 0, axis_index_groups=planes).sum(0)]
    all_to_all x1 -> x0, waiting for transfers between devices: 11.2 us -> none  [per_device(): lax.all_to_all(part.T.reshape(16, 1, 2), both, 0, 0, axis_index_groups=li...]
    pallas_call x2 -> x3, Pallas kernels: 12.1 us -> 20.7 us  [the longest x1 12.6 us: lag_part(): pl.pallas_call(lag_kernel, out_shape=jax.ShapeDtypeStruct((32, 2, 16), F3...]
    ppermute x12 -> x10, starting transfers between devices: 31.4 us -> 39.6 us  [the longest x1 5.4 us: per_device(): own_below = lax.ppermute(own_up, 'flow', up)]
    unnamed x14 -> x22, local copies, waits for them, and re-layouts: 1.27 us -> 7.01 us
  transfers between devices with their start and end apart: 14 -> 11, of which waited for: 5 -> 1; matrix products, arithmetic and copies ran while one was open for 0% -> 2% of each run, Pallas kernels for 0% -> 4%
where the time goes in v2:
time: 131 us
  blocking collectives  56.3 us (43%)
  starting transfers between devices  43.1 us (33%)
  Pallas kernels  20.7 us (16%)
  local copies, waits for them, and re-layouts  7.92 us (6%)
  other arithmetic  2.03 us (2%)
    all_to_all x1, blocking collectives, per_device(): part = lax.all_to_all(part, both, 0, 0, axis_index_groups=planes).sum(0)  30.7 us
    all_to_all x1, blocking collectives, per_device(): lax.all_to_all(part.T.reshape(16, 1, 2), both, 0, 0, axis_index_groups=li...  25.6 us
    pallas_call x1, Pallas kernels, lag_part(): pl.pallas_call(lag_kernel, out_shape=jax.ShapeDtypeStruct((32, 2, 16), F3...  12.6 us
    unnamed x22, local copies, waits for them, and re-layouts  7.01 us
    ppermute x1, starting transfers between devices, per_device(): own_below = lax.ppermute(own_up, 'flow', up)  5.4 us
    ppermute x1, starting transfers between devices, per_device(): other_below = lax.ppermute(other[:25], 'flow', up)  5.1 us
    ppermute x1, starting transfers between devices, per_device(): fwd = lax.ppermute(half1, 'tm', forward)  5.02 us
    ppermute x1, starting transfers between devices, per_device(): other = lax.ppermute(swap, 'tm', pair)  4.82 us
  transfers between devices with their start and end apart: 11, of which 1 were waited for; matrix products, arithmetic and copies ran while one was open for 2% of the time, Pallas kernels for 4%

profile of v2, /device:TPU:1, one launch (start us, length us, event | category | flops | bytes accessed | tf_op | source)
XLA Modules:
  0.0 130.7 jit_solution(8989988246051984045)
XLA Ops:
  0.0 0.0 copy-start
  0.0 1.2 copy-done
  1.2 0.0 copy-start.4
  1.2 0.9 copy-done.4
  2.1 0.0 copy-start.5
  2.1 0.9 copy-done.5
  3.0 0.9 copy-done.6
  3.9 3.3 %split.1 = (bf16[32,64,128]{2,1,0:T(8,128)(2,1)S(1)}, bf16[32,64,128]{2,1,0:T(8,128)(2,1)S(1)}, bf16[32,64,128]{2,1,0:T(8,128)(2,1)S(1)}, bf16[50,64,128]{2,1,0:...) custom-call(s32[1]{0:T(128)} %bitcast.h_ref, ...), custom_call_target="tpu_custom_call" | custom-call | flops 1000000 | bytes 3000000 | tf_op jit(solution)/shard_map/split/pallas_call | solution.py:62
  7.3 1.3 collective-permute-start.6
  8.6 5.0 %collective-permute-start.7 = (bf16[32,64,128]{2,1,0:T(8,128)(2,1)S(1)}, bf16[32,64,128]{2,1,0:T(8,128)(2,1)S(1)}, u32[]{:S(2)}, u32[]{:S(2)}) collective-permute-start(bf16[32,64,128]{2,1,0:T(8,128)(2,1)S(1)} %get-tuple-element.18.half1), channel_id=1, source_target_pairs={{0,2},{1,3},{2,4},{3,5},{4,6},{5,7},{6,8},{7,9},{8,10},{9,11},{10,... | collective-permute-start | bytes 1572872 | tf_op jit(solution)/shard_map/ppermute | solution.py:331
  13.6 4.8 %collective-permute-start.5 = (bf16[32,64,128]{2,1,0:T(8,128)(2,1)S(1)}, bf16[32,64,128]{2,1,0:T(8,128)(2,1)S(1)}, u32[]{:S(2)}, u32[]{:S(2)}) collective-permute-start(bf16[32,64,128]{2,1,0:T(8,128)(2,1)S(1)} %get-tuple-element.26), channel_id=1, source_target_pairs={{0,1},{1,0},{2,3},{3,2},{4,5},{5,4},{6,7},{7,6},{8,9},{9,8},{10,11... | collective-permute-start | bytes 1572872 | tf_op jit(solution)/shard_map/ppermute | solution.py:329
  18.4 5.4 %collective-permute-start.3 = (bf16[50,64,128]{2,1,0:T(8,128)(2,1)}, bf16[50,64,128]{2,1,0:T(8,128)(2,1)S(1)}, u32[]{:S(2)}, u32[]{:S(2)}) collective-permute-start(bf16[50,64,128]{2,1,0:T(8,128)(2,1)} %get-tuple-element.20), channel_id=1, source_target_pairs={{32,0},{64,32},{96,64},{128,96},{160,128},{192,160},{224,192},{256... | collective-permute-start | bytes 2457608 | tf_op jit(solution)/shard_map/ppermute | solution.py:332
  23.8 0.0 collective-permute-done.6.back
  23.9 0.0 collective-permute-done.7.fwd
  23.9 0.8 pad_maximum_fusion
  24.7 4.6 %collective-permute-start.10 = (bf16[26,64,128]{2,1,0:T(8,128)(2,1)}, bf16[26,64,128]{2,1,0:T(8,128)(2,1)}, u32[]{:S(2)}, u32[]{:S(2)}) collective-permute-start(bf16[26,64,128]{2,1,0:T(8,128)(2,1)} %pad_maximum_fusion), channel_id=1, source_target_pairs={{32,0},{64,32},{96,64},{128,96},{160,128},{192,160},{224,192},{256... | collective-permute-start | bytes 1277960 | tf_op jit(solution)/shard_map/ppermute | solution.py:338
  29.4 0.0 collective-permute-done.5.other
  29.4 0.8 slice.27
  30.2 5.1 %collective-permute-start.9 = (bf16[25,64,128]{2,1,0:T(8,128)(2,1)}, bf16[25,64,128]{2,1,0:T(8,128)(2,1)}, u32[]{:S(2)}, u32[]{:S(2)}) collective-permute-start(bf16[25,64,128]{2,1,0:T(8,128)(2,1)} %slice.27), channel_id=1, source_target_pairs={{32,0},{64,32},{96,64},{128,96},{160,128},{192,160},{224,192},{256... | collective-permute-start | bytes 1228808 | tf_op jit(solution)/shard_map/ppermute | solution.py:337
  35.3 0.0 copy-done.1
  35.3 1.9 %collective-permute-start.4 = (f32[2,2,96,128]{3,2,1,0:T(8,128)}, f32[2,2,96,128]{3,2,1,0:T(8,128)S(1)}, u32[]{:S(2)}, u32[]{:S(2)}) collective-permute-start(f32[2,2,96,128]{3,2,1,0:T(8,128)} %get-tuple-element.22), channel_id=1, source_target_pairs={{32,0},{64,32},{96,64},{128,96},{160,128},{192,160},{224,192},{256... | collective-permute-start | bytes 589832 | tf_op jit(solution)/shard_map/ppermute | solution.py:334
  37.2 3.6 %collective-permute-start.2 = (bf16[2,64,128]{2,1,0:T(8,128)(2,1)S(1)}, bf16[2,64,128]{2,1,0:T(8,128)(2,1)S(1)}, u32[]{:S(2)}, u32[]{:S(2)}) collective-permute-start(bf16[2,64,128]{2,1,0:T(8,128)(2,1)S(1)} %get-tuple-element.19), channel_id=1, source_target_pairs={{0,32},{32,64},{64,96},{96,128},{128,160},{160,192},{192,224},{224... | collective-permute-start | bytes 98312 | tf_op jit(solution)/shard_map/ppermute | solution.py:333
  40.9 0.6 pad_maximum_fusion.1
  41.5 0.4 collective-permute-done.2.above
  41.9 0.6 copy-done.7
  42.5 4.2 %collective-permute-start.8 = (bf16[3,64,128]{2,1,0:T(8,128)(2,1)}, bf16[3,64,128]{2,1,0:T(8,128)(2,1)S(1)}, u32[]{:S(2)}, u32[]{:S(2)}) collective-permute-start(bf16[3,64,128]{2,1,0:T(8,128)(2,1)} %pad_maximum_fusion.1), channel_id=1, source_target_pairs={{0,32},{32,64},{64,96},{96,128},{128,160},{160,192},{192,224},{224... | collective-permute-start | bytes 147464 | tf_op jit(solution)/shard_map/ppermute | solution.py:339
  46.7 0.0 copy-start.10
  46.7 0.0 collective-permute-done.4.coef_up
  46.8 3.6 %collective-permute-start = (s32[16]{0:T(128)}, s32[16]{0:T(128)S(1)}, u32[]{:S(2)}, u32[]{:S(2)}) collective-permute-start(s32[16]{0:T(128)} %off_own.1), channel_id=1, source_target_pairs={{0,1},{1,0},{2,3},{3,2},{4,5},{5,4},{6,7},{7,6},{8,9},{9,8},{10,11... | collective-permute-start | bytes 200 | tf_op jit(solution)/shard_map/ppermute | solution.py:335
  50.4 0.0 collective-permute-done.3.below
  50.4 3.5 %collective-permute-start.1 = (s32[16]{0:T(128)}, s32[16]{0:T(128)S(1)}, u32[]{:S(2)}, u32[]{:S(2)}) collective-permute-start(s32[16]{0:T(128)} %off_own.1), channel_id=1, source_target_pairs={{0,2},{1,3},{2,4},{3,5},{4,6},{5,7},{6,8},{7,9},{8,10},{9,11},{10,... | collective-permute-start | bytes 200 | tf_op jit(solution)/shard_map/ppermute | solution.py:336
  53.9 0.0 copy-done.3
  53.9 0.0 copy-start.2
  53.9 1.0 copy-done.2
  54.9 0.8 copy-done.8
  55.7 0.7 copy-done.9
  56.4 4.7 %own.1 = (bf16[2,56,64,128]{3,2,1,0:T(8,128)(2,1)S(1)}, f32[2,32,8,8,128]{4,3,2,1,0:T(8,128)S(1)}, bf16[128,8192]{1,0:T(8,128)(2,1)S(1)}) custom-call(s32[1]{0:T(128)} %bitcast.h_ref, s32[16]{0:T(128)S(1)} %copy-done.9, s32[32,1024]{1,0:T(8,128)S(1)} %copy-done.3, bf16[32,64,128]{2,1,0:T(8,128)(2,1)S(1)} %get-tuple-element.17.half0, ...), custom_call_target="tpu_custom_call" | custom-call | flops 12000000 | bytes 9000000 | tf_op jit(solution)/shard_map/own/pallas_call | solution.py:175
  61.1 0.0 collective-permute-done.off_other
  61.1 0.0 collective-permute-done.1.off_back
  61.1 0.0 collective-permute-done.8.above
  61.1 0.0 collective-permute-done.9.other_below
  61.1 0.0 collective-permute-done.10.two_below
  61.1 0.0 copy-done.10
  61.1 12.6 %lags.1 = f32[32,2,16]{2,1,0:T(2,128)S(1)} custom-call(s32[1]{0:T(128)} %bitcast.h_ref, s32[16]{0:T(128)S(1)} %copy-done.10, s32[16]{0:T(128)S(1)} %collective-permute-done.off_other, s32[16]{0:T(128)S(1)} %collective-permute-done.1.off_back, bf16[2,56,64,128]{3,2,1,0:T(8,128)(2,1)S(1)} %get-tuple-element.23.fixed, ...), custom_call_target="tpu_custom_call" | custom-call | flops 34000000 | bytes 12000000 | tf_op jit(solution)/shard_map/lags/pallas_call | solution.py:300
  73.7 30.7 %all_to_all.10 = f32[32,2,16]{2,1,0:T(2,128)S(1)} all-to-all(f32[32,2,16]{2,1,0:T(2,128)S(1)} %lags.1), channel_id=1, replica_groups={{0,1,32,33,64,65,96,97,128,129,160,161,192,193,224,225,256,257,288,289,..., dimensions={0} | all-to-all | bytes 8192 | tf_op jit(solution)/shard_map/all_to_all | solution.py:360
  104.5 0.1 copy.7
  104.6 25.6 %all_to_all.11 = f32[16,1,2]{2,1,0:T(1,128)S(1)} all-to-all(f32[16,1,2]{2,1,0:T(1,128)S(1)} %copy.7), channel_id=1, replica_groups={{0,2,4,6,8,10,12,14,16,18,20,22,24,26,28,30},{1,3,5,7,9,11,13,15,17,19,..., dimensions={0} | all-to-all | bytes 256 | tf_op jit(solution)/shard_map/all_to_all | solution.py:361
  130.2 0.5 divide_bitcast_fusion
  (12 shorter events, 0.1 us)
Async XLA Ops:
  0.0 1.2 copy-start
  1.2 0.9 copy-start.4
  2.1 0.9 copy-start.5
  3.0 0.9 copy-start.6
  3.9 49.9 %copy-start.3 = (s32[32,1024]{1,0:T(8,128)S(1)}, s32[32,1024]{1,0:T(8,128)}, u32[]{:S(2)}) copy-start(s32[32,1024]{1,0:T(8,128)} %bins_ref.1) | copy-start | bytes 393220
  7.3 28.0 %copy-start.1 = (bf16[32,64,128]{2,1,0:T(8,128)(2,1)}, bf16[32,64,128]{2,1,0:T(8,128)(2,1)S(1)}, u32[]{:S(2)}) copy-start(bf16[32,64,128]{2,1,0:T(8,128)(2,1)S(1)} %get-tuple-element.18.half1) | copy-start | bytes 1572868
  7.3 16.6 %collective-permute-start.6 = (bf16[32,64,128]{2,1,0:T(8,128)(2,1)S(1)}, bf16[32,64,128]{2,1,0:T(8,128)(2,1)S(1)}, u32[]{:S(2)}, u32[]{:S(2)}) collective-permute-start(bf16[32,64,128]{2,1,0:T(8,128)(2,1)S(1)} %get-tuple-element.17.half0), channel_id=1, source_target_pairs={{2,0},{3,1},{4,2},{5,3},{6,4},{7,5},{8,6},{9,7},{10,8},{11,9},{12,... | collective-permute-start | bytes 1572872 | tf_op jit(solution)/shard_map/ppermute | solution.py:330
  8.6 15.3 %collective-permute-start.7 = (bf16[32,64,128]{2,1,0:T(8,128)(2,1)S(1)}, bf16[32,64,128]{2,1,0:T(8,128)(2,1)S(1)}, u32[]{:S(2)}, u32[]{:S(2)}) collective-permute-start(bf16[32,64,128]{2,1,0:T(8,128)(2,1)S(1)} %get-tuple-element.18.half1), channel_id=1, source_target_pairs={{0,2},{1,3},{2,4},{3,5},{4,6},{5,7},{6,8},{7,9},{8,10},{9,11},{10,... | collective-permute-start | bytes 1572872 | tf_op jit(solution)/shard_map/ppermute | solution.py:331
  13.6 15.8 %collective-permute-start.5 = (bf16[32,64,128]{2,1,0:T(8,128)(2,1)S(1)}, bf16[32,64,128]{2,1,0:T(8,128)(2,1)S(1)}, u32[]{:S(2)}, u32[]{:S(2)}) collective-permute-start(bf16[32,64,128]{2,1,0:T(8,128)(2,1)S(1)} %get-tuple-element.26), channel_id=1, source_target_pairs={{0,1},{1,0},{2,3},{3,2},{4,5},{5,4},{6,7},{7,6},{8,9},{9,8},{10,11... | collective-permute-start | bytes 1572872 | tf_op jit(solution)/shard_map/ppermute | solution.py:329
  18.4 31.9 %collective-permute-start.3 = (bf16[50,64,128]{2,1,0:T(8,128)(2,1)}, bf16[50,64,128]{2,1,0:T(8,128)(2,1)S(1)}, u32[]{:S(2)}, u32[]{:S(2)}) collective-permute-start(bf16[50,64,128]{2,1,0:T(8,128)(2,1)} %get-tuple-element.20), channel_id=1, source_target_pairs={{32,0},{64,32},{96,64},{128,96},{160,128},{192,160},{224,192},{256... | collective-permute-start | bytes 2457608 | tf_op jit(solution)/shard_map/ppermute | solution.py:332
  24.7 36.4 %collective-permute-start.10 = (bf16[26,64,128]{2,1,0:T(8,128)(2,1)}, bf16[26,64,128]{2,1,0:T(8,128)(2,1)}, u32[]{:S(2)}, u32[]{:S(2)}) collective-permute-start(bf16[26,64,128]{2,1,0:T(8,128)(2,1)} %pad_maximum_fusion), channel_id=1, source_target_pairs={{32,0},{64,32},{96,64},{128,96},{160,128},{192,160},{224,192},{256... | collective-permute-start | bytes 1277960 | tf_op jit(solution)/shard_map/ppermute | solution.py:338
  30.2 30.9 %collective-permute-start.9 = (bf16[25,64,128]{2,1,0:T(8,128)(2,1)}, bf16[25,64,128]{2,1,0:T(8,128)(2,1)}, u32[]{:S(2)}, u32[]{:S(2)}) collective-permute-start(bf16[25,64,128]{2,1,0:T(8,128)(2,1)} %slice.27), channel_id=1, source_target_pairs={{32,0},{64,32},{96,64},{128,96},{160,128},{192,160},{224,192},{256... | collective-permute-start | bytes 1228808 | tf_op jit(solution)/shard_map/ppermute | solution.py:337
  35.3 11.5 %collective-permute-start.4 = (f32[2,2,96,128]{3,2,1,0:T(8,128)}, f32[2,2,96,128]{3,2,1,0:T(8,128)S(1)}, u32[]{:S(2)}, u32[]{:S(2)}) collective-permute-start(f32[2,2,96,128]{3,2,1,0:T(8,128)} %get-tuple-element.22), channel_id=1, source_target_pairs={{32,0},{64,32},{96,64},{128,96},{160,128},{192,160},{224,192},{256... | collective-permute-start | bytes 589832 | tf_op jit(solution)/shard_map/ppermute | solution.py:334
  37.2 4.7 %collective-permute-start.2 = (bf16[2,64,128]{2,1,0:T(8,128)(2,1)S(1)}, bf16[2,64,128]{2,1,0:T(8,128)(2,1)S(1)}, u32[]{:S(2)}, u32[]{:S(2)}) collective-permute-start(bf16[2,64,128]{2,1,0:T(8,128)(2,1)S(1)} %get-tuple-element.19), channel_id=1, source_target_pairs={{0,32},{32,64},{64,96},{96,128},{128,160},{160,192},{192,224},{224... | collective-permute-start | bytes 98312 | tf_op jit(solution)/shard_map/ppermute | solution.py:333
  41.9 0.6 copy-start.7
  42.5 18.6 %collective-permute-start.8 = (bf16[3,64,128]{2,1,0:T(8,128)(2,1)}, bf16[3,64,128]{2,1,0:T(8,128)(2,1)S(1)}, u32[]{:S(2)}, u32[]{:S(2)}) collective-permute-start(bf16[3,64,128]{2,1,0:T(8,128)(2,1)} %pad_maximum_fusion.1), channel_id=1, source_target_pairs={{0,32},{32,64},{64,96},{96,128},{128,160},{160,192},{192,224},{224... | collective-permute-start | bytes 147464 | tf_op jit(solution)/shard_map/ppermute | solution.py:339
  46.7 14.4 %copy-start.10 = (s32[16]{0:T(128)S(1)}, s32[16]{0:T(128)}, u32[]{:S(2)}) copy-start(s32[16]{0:T(128)} %off_own.1) | copy-start | bytes 196
  46.8 14.3 %collective-permute-start = (s32[16]{0:T(128)}, s32[16]{0:T(128)S(1)}, u32[]{:S(2)}, u32[]{:S(2)}) collective-permute-start(s32[16]{0:T(128)} %off_own.1), channel_id=1, source_target_pairs={{0,1},{1,0},{2,3},{3,2},{4,5},{5,4},{6,7},{7,6},{8,9},{9,8},{10,11... | collective-permute-start | bytes 200 | tf_op jit(solution)/shard_map/ppermute | solution.py:335
  50.4 10.7 %collective-permute-start.1 = (s32[16]{0:T(128)}, s32[16]{0:T(128)S(1)}, u32[]{:S(2)}, u32[]{:S(2)}) collective-permute-start(s32[16]{0:T(128)} %off_own.1), channel_id=1, source_target_pairs={{0,2},{1,3},{2,4},{3,5},{4,6},{5,7},{6,8},{7,9},{8,10},{9,11},{10,... | collective-permute-start | bytes 200 | tf_op jit(solution)/shard_map/ppermute | solution.py:336
  53.9 1.0 copy-start.2
  54.9 0.8 copy-start.8
  55.7 0.7 copy-start.9

commit v3 on v1

v3 whole, which is shorter than its diff:
```python
import jax
import jax.numpy as jnp
from jax import lax
from jax.experimental import pallas as pl
from jax.experimental.pallas import tpu as pltpu
from jax.sharding import PartitionSpec as P

OFF_MAX = 24
Q = 32
F32, BF16 = jnp.float32, jnp.bfloat16
VMEM = pl.BlockSpec(memory_space=pltpu.VMEM)
SMEM = pl.BlockSpec(memory_space=pltpu.SMEM)
HBM = pl.BlockSpec(memory_space=pltpu.HBM)
NT = (((1,), (1,)), ((), ()))


def correct_kernel(
    h_ref, off_ref, up_ref, dn_ref, f_hbm, gain_hbm, couple_hbm, mask_hbm,
    back, fwd, swap, own_up, raw, done, f_ref, gain_ref, couple_ref, mask_ref, sems,
):
    h = h_ref[0]
    pairs = (
        (f_hbm, f_ref), (gain_hbm, gain_ref), (couple_hbm, couple_ref), (mask_hbm, mask_ref)
    )
    copies = [pltpu.make_async_copy(a, b, sems.at[i]) for i, (a, b) in enumerate(pairs)]
    for copy in copies:
        copy.start()
    for copy in copies:
        copy.wait()

    @pl.loop(0, 16)
    def _(f):
        for j in range(8):
            cols = slice(128 * j, 128 * j + 128)
            for k in range(2):
                raw[f, j, 8 + 16 * k : 24 + 16 * k, :] = f_ref[
                    f, 16 * k : 16 * k + 16, cols
                ].astype(F32)

    for f in range(16):
        for j in range(8):
            cols = slice(128 * j, 128 * j + 128)
            raw[f, j, 7:8, :] = up_ref[f : f + 1, cols].astype(F32)
            raw[f, j, 40:41, :] = dn_ref[f : f + 1, cols].astype(F32)

    @pl.loop(0, 16)
    def _(f):
        for j in range(8):
            cols = slice(128 * j, 128 * j + 128)
            for k in range(4):
                rows = slice(8 * k, 8 * k + 8)
                here = raw[f, j, 8 * k + 8 : 8 * k + 16, :]
                above = raw[f, j, 8 * k + 7 : 8 * k + 15, :]
                below = raw[f, j, 8 * k + 9 : 8 * k + 17, :]
                value = gain_ref[rows, cols] * here + couple_ref[rows, cols] * (above + below)
                value = value * mask_ref[rows, cols].astype(F32)
                start = (j // 4) * 2048 + k * 512 + (j % 4) + 4 * f
                done[pl.ds(start, 8, stride=64), :] = value

    def row_of(half, r):
        return done[pl.ds(pl.multiple_of(half * 2048 + r * 64, 64), 64), :].astype(BF16)

    @pl.loop(0, 24)
    def _(r):
        first, second = row_of(0, r), row_of(1, r)
        back[r], fwd[r], swap[r] = first, second, row_of(1 - h, r)
        own_up[r], own_up[r + 24] = first, second

    @pl.loop(24, 32)
    def _(r):
        back[r], fwd[r], swap[r] = row_of(0, r), row_of(1, r), row_of(1 - h, r)

    frame = lax.broadcasted_iota(jnp.int32, (64, 128), 0) >> 2
    offs = jnp.zeros((64, 128), jnp.int32)
    for f in range(16):
        offs = jnp.where(frame == f, off_ref[f], offs)
    offs = offs.astype(F32).astype(BF16)
    fwd[32], swap[32] = offs, offs


def correct(h, off, frames, up, dn, gain, couple, mask):
    shapes = tuple(jax.ShapeDtypeStruct((n, 64, 128), BF16) for n in (32, 33, 33, 48))
    return pl.pallas_call(
        correct_kernel,
        out_shape=shapes,
        in_specs=[SMEM] * 2 + [VMEM] * 2 + [HBM] * 4,
        out_specs=(VMEM,) * 4,
        scratch_shapes=[
            pltpu.VMEM((16, 8, 48, 128), F32),
            pltpu.VMEM((2 * 32 * 64, 128), F32),
            pltpu.VMEM((16, 32, 1024), BF16),
            pltpu.VMEM((32, 1024), F32),
            pltpu.VMEM((32, 1024), F32),
            pltpu.VMEM((32, 1024), jnp.int32),
            pltpu.SemaphoreType.DMA((4,)),
        ],
        name="correct",
        cost_estimate=pl.CostEstimate(flops=4000000, bytes_accessed=3000000, transcendentals=0),
        compiler_params=pltpu.CompilerParams(vmem_limit_bytes=63100 << 10),
    )(h, off, up, dn, frames, gain, couple, mask)


def low_half():
    return lax.broadcasted_iota(jnp.int32, (8, 128), 0) < 4


def twice(pair, swap, odd, low):
    return jnp.where(low, swap, pair) if odd else jnp.where(low, pair, swap)


def table_kernel(h_ref, bins_ref, table):
    h = h_ref[0]
    bin_id = lax.broadcasted_iota(jnp.int32, (32, 128), 0)
    for role in range(2):

        @pl.loop(0, 4)
        def _(r8, role=role):
            half = h if role == 0 else 1 - h
            for g in range(4):
                lane = pl.multiple_of(half * 512 + g * 128, 128)
                bins = bins_ref[pl.ds(pl.multiple_of(r8 * 8, 8), 8), pl.ds(lane, 128)]
                for i in range(8):
                    at = pl.multiple_of(role * 4096 + r8 * 1024 + i * 128, 128)
                    hit = jnp.where(bins[i : i + 1] == bin_id, 1.0, 0.0)
                    table[32 * g : 32 * g + 32, pl.ds(at, 128)] = hit.astype(BF16)


def bin_table(h, bins):
    return pl.pallas_call(
        table_kernel,
        out_shape=jax.ShapeDtypeStruct((128, 8192), BF16),
        in_specs=[SMEM, VMEM],
        out_specs=VMEM,
        name="table",
        cost_estimate=pl.CostEstimate(flops=1000000, bytes_accessed=2000000, transcendentals=0),
        compiler_params=pltpu.CompilerParams(vmem_limit_bytes=6 << 20),
    )(h, bins)


def own_kernel(
    h_ref, off_ref, half0, half1, below, acc_ref, work
):
    h = h_ref[0]
    low = low_half()
    work[:, :, 64:72, :] = jnp.zeros((2, 56, 8, 128), F32)
    for half, main in enumerate((half0, half1)):
        role = h if half == 0 else 1 - h

        @pl.loop(0, 32)
        def _(r, main=main, role=role):
            work[role, r, 0:64, :] = main[r].astype(F32)

        @pl.loop(0, 24)
        def _(r, half=half, role=role):
            work[role, r + 32, 0:64, :] = below[24 * half + r].astype(F32)

    for role in range(2):

        @pl.loop(0, 32)
        def _(r, role=role):
            acc = [jnp.zeros((8, 128), F32) for _ in range(8)]
            for k in range(8):
                pair = work[role, r, 8 * k : 8 * k + 8, :]
                swap = pltpu.roll(pair, 4, 0)
                for odd in range(2):
                    t = 2 * k + odd
                    now = twice(pair, swap, odd, low)
                    row = r + off_ref[t]
                    for j in range((16 - t) // 2):
                        at = 4 * (t + 1 + 2 * j)
                        acc[j] = acc[j] + now * work[role, row, at : at + 8, :]
            for j in range(8):
                acc_ref[role, r, j] = acc[j]


def own_part(h, off, half0, half1, below):
    return pl.pallas_call(
        own_kernel,
        out_shape=jax.ShapeDtypeStruct((2, 32, 8, 8, 128), F32),
        in_specs=[SMEM] * 2 + [VMEM] * 3,
        out_specs=VMEM,
        scratch_shapes=[pltpu.VMEM((2, 56, 72, 128), F32)],
        name="own",
        cost_estimate=pl.CostEstimate(flops=8000000, bytes_accessed=7000000, transcendentals=0),
        compiler_params=pltpu.CompilerParams(vmem_limit_bytes=20 << 20),
    )(h, off, half0, half1, below)


def pack_kernel(other, back, two):
    @pl.loop(0, 24)
    def _(r):
        two[r] = other[r]
        two[r + 24] = back[r]


def pack(other, back):
    return pl.pallas_call(
        pack_kernel,
        out_shape=jax.ShapeDtypeStruct((48, 64, 128), BF16),
        in_specs=[VMEM] * 2,
        out_specs=VMEM,
        name="pack",
        cost_estimate=pl.CostEstimate(flops=0, bytes_accessed=1600000, transcendentals=0),
        compiler_params=pltpu.CompilerParams(vmem_limit_bytes=4 << 20),
    )(other, back)


def add_from(acc, later, off, r, source, target, off_at, first_lag, last_lag):
    low = low_half()
    for k in range(8):
        pair = later[r, source + 8 * k : source + 8 * k + 8, :]
        swap = pltpu.roll(pair, 4, 0)
        for odd in range(2):
            i = 2 * k + odd
            now = twice(pair, swap, odd, low)
            row = r + off[off_at + i]
            first, last = first_lag - i, last_lag(i)
            for j in range((first - 1) // 2, (last - 1) // 2 + 1):
                x = now
                if 2 * j + 1 < first:
                    x = jnp.where(low, 0.0, x)
                if 2 * j + 2 > last:
                    x = jnp.where(low, x, 0.0)
                at = target + 4 * (2 * j + 1 - first)
                acc[j] = acc[j] + x * later[row, at : at + 8, :]


def all_lags(later, off, acc_ref, sums, r, at, rows):
    zero = jnp.zeros((8, 128), F32)

    def store(acc, at):
        at = pl.multiple_of(at, 128)
        for j in range(8):
            two = jnp.concatenate([acc[2 * j], acc[2 * j + 1]], 0)
            high = two.astype(BF16)
            sums[16 * j : 16 * j + 16, pl.ds(at, 128)] = high
            rest = (two - high.astype(F32)).astype(BF16)
            sums[128 + 16 * j : 144 + 16 * j, pl.ds(at, 128)] = rest

    acc = [acc_ref[0, r, j] for j in range(8)] + [zero] * 8
    add_from(acc, later, off, r, 0, 64, 0, 16, lambda i: 32)
    add_from(acc, later, off, r, 64, 128, 16, 16, lambda i: 31 - i)
    store(acc, at)
    acc = [acc_ref[1, r, j] for j in range(8)] + [zero] * 8
    add_from(acc, later, off, r, 192, 256, 48, 32, lambda i: 32)
    store(acc, rows * 128 + at)


EARLY = 32 - OFF_MAX


def early_kernel(
    h_ref, off_own, acc_ref, half0, half1, own_below, other, back, fwd,
    later, sums, off, off_rows, off_read, sem,
):
    h = h_ref[0]
    off_rows[0] = other[32].astype(F32).astype(jnp.int32)
    off_rows[1] = fwd[32].astype(F32).astype(jnp.int32)
    read = pltpu.make_async_copy(off_rows, off_read, sem)
    read.start()
    at_half = [pl.multiple_of(192 * h, 64), pl.multiple_of(256 - 128 * h, 64)]
    at_back = pl.multiple_of(128 + 128 * h, 64)
    at_fwd = pl.multiple_of(192 - 192 * h, 64)
    later[:, 320:328, :] = jnp.zeros((56, 8, 128), F32)

    @pl.loop(0, 32)
    def _(r):
        later[r, pl.ds(at_half[0], 64), :] = half0[r].astype(F32)
        later[r, pl.ds(at_half[1], 64), :] = half1[r].astype(F32)
        later[r, 64:128, :] = other[r].astype(F32)
        later[r, pl.ds(at_back, 64), :] = back[r].astype(F32)
        later[r, pl.ds(at_fwd, 64), :] = fwd[r].astype(F32)

    @pl.loop(0, 24)
    def _(r):
        later[r + 32, pl.ds(at_half[0], 64), :] = own_below[r].astype(F32)
        later[r + 32, pl.ds(at_half[1], 64), :] = own_below[r + 24].astype(F32)
        later[r + 32, pl.ds(at_fwd, 64), :] = jnp.zeros((64, 128), F32)

    read.wait()
    for k in range(16):
        off[48 * h + k] = off_own[k]
        off[16 + k] = off_read[0, 4 * k, 0]
        off[48 - 48 * h + k] = off_read[1, 4 * k, 0]

    @pl.loop(0, EARLY)
    def _(r):
        all_lags(later, off, acc_ref, sums, r, r * 128, EARLY)


def early_part(h, off, acc, blocks):
    return pl.pallas_call(
        early_kernel,
        out_shape=(
            jax.ShapeDtypeStruct((56, 328, 128), F32),
            jax.ShapeDtypeStruct((256, 2 * EARLY * 128), BF16),
            jax.ShapeDtypeStruct((64,), jnp.int32),
        ),
        in_specs=[SMEM] * 2 + [VMEM] * 7,
        out_specs=(VMEM, VMEM, SMEM),
        scratch_shapes=[
            pltpu.VMEM((2, 64, 128), jnp.int32),
            pltpu.SMEM((2, 64, 128), jnp.int32),
            pltpu.SemaphoreType.DMA,
        ],
        name="early",
        cost_estimate=pl.CostEstimate(flops=8000000, bytes_accessed=12000000, transcendentals=0),
        compiler_params=pltpu.CompilerParams(vmem_limit_bytes=16 << 20),
    )(h, off, acc, *blocks)


def late_kernel(h_ref, off, later_in, acc_ref, table, sums_early, two_below, later, out_ref, sums):
    h = h_ref[0]
    at_back = pl.multiple_of(128 + 128 * h, 64)

    @pl.loop(0, 24)
    def _(r):
        later[r + 32, 64:128, :] = two_below[r].astype(F32)
        later[r + 32, pl.ds(at_back, 64), :] = two_below[r + 24].astype(F32)

    rows = 32 - EARLY

    @pl.loop(EARLY, 32)
    def _(r):
        all_lags(later, off, acc_ref, sums, r, (r - EARLY) * 128, rows)

    both = jnp.zeros((256, 128), F32)
    for role in range(2):
        for ref, first, count in ((sums_early, 0, EARLY), (sums, EARLY, rows)):
            left = ref[:, role * count * 128 : (role + 1) * count * 128]
            start = role * 4096 + first * 128
            right = table[:, start : start + count * 128]
            both = both + lax.dot_general(left, right, NT, preferred_element_type=F32)
    both = both[:128] + both[128:]
    row = lax.broadcasted_iota(jnp.int32, (128, 128), 0)
    col = lax.broadcasted_iota(jnp.int32, (128, 128), 1)
    both = jnp.where((row & 3) == (col >> 5), both, 0.0)
    q = lax.broadcasted_iota(jnp.int32, (32, 128), 0)
    lane = lax.broadcasted_iota(jnp.int32, (32, 128), 1)
    pick_q = jnp.where((lane & 31) == q, 1.0, 0.0)
    per_q = lax.dot_general(
        pick_q, both, NT, precision=lax.Precision.HIGHEST, preferred_element_type=F32
    )
    z = lax.broadcasted_iota(jnp.int32, (16, 128), 0)
    lane = lax.broadcasted_iota(jnp.int32, (16, 128), 1)
    for side in range(2):
        pick_l = jnp.where((lane >> 2) == 2 * z + side, 1.0, 0.0)
        part = lax.dot_general(
            per_q, pick_l, NT, precision=lax.Precision.HIGHEST, preferred_element_type=F32
        )
        for f in range(16):
            out_ref[2 * f + side] = part[2 * f : 2 * f + 2, :]


def late_part(h, off, later, acc, table, sums, two_below):
    return pl.pallas_call(
        late_kernel,
        out_shape=(
            jax.ShapeDtypeStruct((56, 328, 128), F32),
            jax.ShapeDtypeStruct((32, 2, 16), F32),
        ),
        in_specs=[SMEM] * 2 + [VMEM] * 5,
        out_specs=(VMEM,) * 2,
        input_output_aliases={2: 0},
        scratch_shapes=[pltpu.VMEM((256, 2 * (32 - EARLY) * 128), BF16)],
        name="late",
        cost_estimate=pl.CostEstimate(flops=24000000, bytes_accessed=12000000, transcendentals=0),
        compiler_params=pltpu.CompilerParams(vmem_limit_bytes=16 << 20),
    )(h, off, later, acc, table, sums, two_below)[1]


def device_program(frames, pixel_gain, couple, bin_index, pixel_mask, offsets):
    flow_count, time_count = lax.axis_size("flow"), lax.axis_size("tm")
    down = [(i, i + 1) for i in range(flow_count - 1)]
    up = [(i + 1, i) for i in range(flow_count - 1)]
    pair = [(i, i ^ 1) for i in range(time_count)]
    backward = [(i + 2, i) for i in range(time_count - 2)]
    forward = [(i, i + 2) for i in range(time_count - 2)]
    h = (lax.axis_index("tm") % 2).astype(jnp.int32).reshape(1)

    above = lax.ppermute(frames[:, 31, :], "flow", down)
    below = lax.ppermute(frames[:, 0, :], "flow", up)
    half0, half1, swap, own_up = correct(
        h, offsets, frames, above, below, pixel_gain, couple, pixel_mask
    )
    table = bin_table(h, bin_index)
    other = lax.ppermute(swap, "tm", pair)
    back = lax.ppermute(half0, "tm", backward)
    fwd = lax.ppermute(half1, "tm", forward)
    own_below = lax.ppermute(own_up, "flow", up)
    acc = own_part(h, offsets, half0, half1, own_below)
    two_below = lax.ppermute(pack(other, back), "flow", up)
    later, sums, off = early_part(
        h, offsets, acc, (half0, half1, own_below, other, back, fwd)
    )
    part = late_part(h, off, later, acc, table, sums, two_below)
    both = ("flow", "tm")
    planes = [
        [f * time_count + 2 * z + s for f in range(flow_count) for s in range(2)]
        for z in range(time_count // 2)
    ]
    lines = [
        [f * time_count + 2 * z + s for z in range(time_count // 2)]
        for f in range(flow_count)
        for s in range(2)
    ]
    lag = (lax.axis_index("tm") + 1).astype(F32)
    normaliser = jnp.sqrt((16 * time_count - lag) * (32 * flow_count * 1024 / Q))
    part, normaliser = lax.optimization_barrier((part, normaliser))
    part = lax.all_to_all(part, both, 0, 0, axis_index_groups=planes).sum(0)
    part = lax.all_to_all(part.T.reshape(16, 1, 2), both, 0, 0, axis_index_groups=lines).sum(0)
    return part.reshape(2, 1) / normaliser


def solution(mesh):
    in_specs = (
        P("tm", "flow", None),
        P("flow", None),
        P("flow", None),
        P("flow", None),
        P("flow", None),
        P("tm"),
    )
    return jax.shard_map(
        device_program, mesh=mesh, in_specs=in_specs, out_specs=P("flow", "tm"), check_vma=False
    )
```

time: 116 us -> 113 us (0.974)
  starting transfers between devices: 51.6 us -> 22.8 us
  blocking collectives: 16.4 us -> 42.9 us
  waiting for transfers between devices: 30.9 us -> 15.7 us
  Pallas kernels: 12.1 us -> 22.5 us
  local copies, waits for them, and re-layouts: 3.14 us -> 7.58 us
    all_to_all x1 -> x2, blocking collectives: 16.4 us -> 42.9 us  [the longest x1 27.7 us: device_program(): lax.all_to_all(part.T.reshape(16, 1, 2), both, 0, 0, axis_index_groups=li...]
    all_to_all x1 -> x0, starting transfers between devices: 16.3 us -> none  [per_device(): lax.all_to_all(part.T.reshape(16, 1, 2), both, 0, 0, axis_index_groups=li...]
    ppermute x13 -> x7, starting transfers between devices: 35.2 us -> 22.8 us  [the longest x1 5.54 us: device_program(): below = lax.ppermute(frames[:, 0, :], 'flow', up)]
    all_to_all x1 -> x0, waiting for transfers between devices: 11.2 us -> none  [per_device(): lax.all_to_all(part.T.reshape(16, 1, 2), both, 0, 0, axis_index_groups=li...]
    pallas_call x2 -> x6, Pallas kernels: 12.1 us -> 22.5 us  [the longest x1 7.56 us: late_part(): pl.pallas_call(late_kernel, out_shape=(jax.ShapeDtypeStruct((56, 328, 128...]
    unnamed x14 -> x18, local copies, waits for them, and re-layouts: 1.27 us -> 6.36 us
    ppermute x13 -> x7, waiting for transfers between devices: 19.7 us -> 15.7 us  [the longest x1 11.6 us: device_program(): back = lax.ppermute(half0, 'tm', backward)]
  transfers between devices with their start and end apart: 14 -> 7, of which waited for: 5 -> 3; matrix products, arithmetic and copies ran while one was open for 0% -> 0% of each run, Pallas kernels for 0% -> 8%
where the time goes in v3:
time: 113 us; the launch traced here: 112 us
  blocking collectives  42.9 us (38%)
  starting transfers between devices  22.8 us (20%)
  Pallas kernels  22.5 us (20%)
  waiting for transfers between devices  15.7 us (14%)
  local copies, waits for them, and re-layouts  7.58 us (7%)
    all_to_all x1, blocking collectives, device_program(): lax.all_to_all(part.T.reshape(16, 1, 2), both, 0, 0, axis_index_groups=li...  27.7 us
    all_to_all x1, blocking collectives, device_program(): part = lax.all_to_all(part, both, 0, 0, axis_index_groups=planes).sum(0)  15.2 us
    ppermute x1, waiting for transfers between devices, device_program(): back = lax.ppermute(half0, 'tm', backward)  11.6 us
    pallas_call x1, Pallas kernels, late_part(): pl.pallas_call(late_kernel, out_shape=(jax.ShapeDtypeStruct((56, 328, 128...  7.56 us
    pallas_call x1, Pallas kernels, correct(): pl.pallas_call(correct_kernel, out_shape=shapes, in_specs=[SMEM] * 2 + [V...  6.38 us
    unnamed x18, local copies, waits for them, and re-layouts  6.36 us
    ppermute x1, starting transfers between devices, device_program(): below = lax.ppermute(frames[:, 0, :], 'flow', up)  5.54 us
    pallas_call x1, Pallas kernels, early_part(): pl.pallas_call(early_kernel, out_shape=(jax.ShapeDtypeStruct((56, 328, 12...  4.99 us
  transfers between devices with their start and end apart: 7, of which 3 were waited for; matrix products, arithmetic and copies ran while one was open for 0% of the time, Pallas kernels for 8%

profile of v3, /device:TPU:1, one launch (start us, length us, event | category | flops | bytes accessed | tf_op | source)
XLA Modules:
  0.0 112.4 jit_solution(947964977920483306)
XLA Ops:
  0.0 1.1 %fusion = (bf16[16,1,1024]{2,1,0:T(2,128)(2,1)S(1)}, bf16[16,1,1024]{2,1,0:T(2,128)(2,1)S(1)}) fusion(bf16[16,32,1024]{2,1,0:T(8,128)(2,1)} %f_hbm.1), kind=kLoop, calls=%fused_computation.3 | loop fusion | bytes 131072 | tf_op jit(solution)/shard_map/slice | solution.py:382
  1.2 4.5 %collective-permute-start = (bf16[16,1024]{1,0:T(8,128)(2,1)S(1)}, bf16[16,1024]{1,0:T(8,128)(2,1)S(1)}, u32[]{:S(2)}, u32[]{:S(2)}) collective-permute-start(bf16[16,1024]{1,0:T(8,128)(2,1)S(1)} %bitcast.12), channel_id=1, source_target_pairs={{0,32},{32,64},{64,96},{96,128},{128,160},{160,192},{192,224},{224... | collective-permute-start | bytes 98312 | tf_op jit(solution)/shard_map/ppermute | solution.py:381
  5.7 5.5 %collective-permute-start.1 = (bf16[16,1024]{1,0:T(8,128)(2,1)S(1)}, bf16[16,1024]{1,0:T(8,128)(2,1)S(1)}, u32[]{:S(2)}, u32[]{:S(2)}) collective-permute-start(bf16[16,1024]{1,0:T(8,128)(2,1)S(1)} %bitcast.13), channel_id=1, source_target_pairs={{32,0},{64,32},{96,64},{128,96},{160,128},{192,160},{224,192},{256... | collective-permute-start | bytes 98312 | tf_op jit(solution)/shard_map/ppermute | solution.py:382
  11.2 0.0 collective-permute-done.up_ref
  11.3 0.0 copy-start.6
  11.3 0.8 collective-permute-done.1.dn_ref
  12.1 0.0 copy-start.7
  12.1 0.0 copy-done.6
  12.1 0.6 copy-done.7
  12.7 6.4 %correct.1 = (bf16[32,64,128]{2,1,0:T(8,128)(2,1)}, bf16[33,64,128]{2,1,0:T(8,128)(2,1)}, bf16[33,64,128]{2,1,0:T(8,128)(2,1)}, bf16[48,64,128]{2,1,0:T(8,128)(2,1)}) custom-call(s32[1]{0:T(128)} %bitcast.h_ref, s32[16]{0:T(128)} %off_own.1, bf16[16,1024]{1,0:T(8,128)(2,1)} %copy-done.6, bf16[16,1024]{1,0:T(8,128)(2,1)} %copy-done.7, ...), custom_call_target="tpu_custom_call" | custom-call | flops 4000000 | bytes 3000000 | tf_op jit(solution)/shard_map/correct/pallas_call | solution.py:83
  19.1 3.7 %collective-permute-start.3 = (bf16[33,64,128]{2,1,0:T(8,128)(2,1)}, bf16[33,64,128]{2,1,0:T(8,128)(2,1)S(1)}, u32[]{:S(2)}, u32[]{:S(2)}) collective-permute-start(bf16[33,64,128]{2,1,0:T(8,128)(2,1)} %get-tuple-element.18), channel_id=1, source_target_pairs={{0,1},{1,0},{2,3},{3,2},{4,5},{5,4},{6,7},{7,6},{8,9},{9,8},{10,11... | collective-permute-start | bytes 1622024 | tf_op jit(solution)/shard_map/ppermute | solution.py:387
  22.7 1.3 %collective-permute-start.4 = (bf16[32,64,128]{2,1,0:T(8,128)(2,1)}, bf16[32,64,128]{2,1,0:T(8,128)(2,1)S(1)}, u32[]{:S(2)}, u32[]{:S(2)}) collective-permute-start(bf16[32,64,128]{2,1,0:T(8,128)(2,1)} %get-tuple-element.15.half0), channel_id=1, source_target_pairs={{2,0},{3,1},{4,2},{5,3},{6,4},{7,5},{8,6},{9,7},{10,8},{11,9},{12,... | collective-permute-start | bytes 1572872 | tf_op jit(solution)/shard_map/ppermute | solution.py:388
  24.0 1.9 %collective-permute-start.2 = (bf16[48,64,128]{2,1,0:T(8,128)(2,1)}, bf16[48,64,128]{2,1,0:T(8,128)(2,1)S(1)}, u32[]{:S(2)}, u32[]{:S(2)}) collective-permute-start(bf16[48,64,128]{2,1,0:T(8,128)(2,1)} %get-tuple-element.17), channel_id=1, source_target_pairs={{32,0},{64,32},{96,64},{128,96},{160,128},{192,160},{224,192},{256... | collective-permute-start | bytes 2359304 | tf_op jit(solution)/shard_map/ppermute | solution.py:390
  26.0 11.6 %collective-permute-done.4.back = bf16[32,64,128]{2,1,0:T(8,128)(2,1)S(1)} collective-permute-done((bf16[32,64,128]{2,1,0:T(8,128)(2,1)}, bf16[32,64,128]{2,1,0:T(8,128)(2,1)S(1)}, u32[]{:S(2)}, u32[]{:S(2)}) %collective-permute-start.4) | collective-permute-done | bytes 524320 | tf_op jit(solution)/shard_map/ppermute | solution.py:388
  37.6 0.0 collective-permute-done.3.other
  37.6 0.1 pack.1
  37.7 1.9 %collective-permute-start.6 = (bf16[48,64,128]{2,1,0:T(8,128)(2,1)S(1)}, bf16[48,64,128]{2,1,0:T(8,128)(2,1)S(1)}, u32[]{:S(2)}, u32[]{:S(2)}) collective-permute-start(bf16[48,64,128]{2,1,0:T(8,128)(2,1)S(1)} %pack.1), channel_id=1, source_target_pairs={{32,0},{64,32},{96,64},{128,96},{160,128},{192,160},{224,192},{256... | collective-permute-start | bytes 2359304 | tf_op jit(solution)/shard_map/ppermute | solution.py:392
  39.6 3.9 %collective-permute-start.5 = (bf16[33,64,128]{2,1,0:T(8,128)(2,1)}, bf16[33,64,128]{2,1,0:T(8,128)(2,1)}, u32[]{:S(2)}, u32[]{:S(2)}) collective-permute-start(bf16[33,64,128]{2,1,0:T(8,128)(2,1)} %get-tuple-element.16.half1), channel_id=1, source_target_pairs={{0,2},{1,3},{2,4},{3,5},{4,6},{5,7},{6,8},{7,9},{8,10},{9,11},{10,... | collective-permute-start | bytes 1622024 | tf_op jit(solution)/shard_map/ppermute | solution.py:389
  43.6 0.0 copy-start.4
  43.6 0.9 copy-done.4
  44.5 0.6 table.1
  45.1 0.0 collective-permute-done.2.below.own_below
  45.1 0.0 copy-start
  45.1 1.0 copy-done
  46.2 0.0 copy-start.2
  46.2 1.0 copy-done.2
  47.2 0.0 copy-start.5
  47.2 0.7 copy-done.5
  47.9 2.9 %own.1.acc_ref = f32[2,32,8,8,128]{4,3,2,1,0:T(8,128)S(1)} custom-call(s32[1]{0:T(128)} %bitcast.h_ref, s32[16]{0:T(128)S(1)} %copy-done.5, bf16[32,64,128]{2,1,0:T(8,128)(2,1)S(1)} %copy-done.2, bf16[33,64,128]{2,1,0:T(8,128)(2,1)S(1)} %copy-done, bf16[48,64,128]{2,1,0:T(8,128)(2,1)S(1)} %collective-permute-done.2.below.own_below), custom_call_target="tpu_custom_call" | custom-call | flops 8000000 | bytes 7000000 | tf_op jit(solution)/shard_map/own/pallas_call | solution.py:177
  50.8 3.3 %collective-permute-done.5.fwd = bf16[33,64,128]{2,1,0:T(8,128)(2,1)} collective-permute-done((bf16[33,64,128]{2,1,0:T(8,128)(2,1)}, bf16[33,64,128]{2,1,0:T(8,128)(2,1)}, u32[]{:S(2)}, u32[]{:S(2)}) %collective-permute-start.5) | collective-permute-done | bytes 540704 | tf_op jit(solution)/shard_map/ppermute | solution.py:389
  54.1 0.0 copy-start.1
  54.1 1.0 copy-done.1
  55.1 0.0 copy-start.3
  55.1 1.0 copy-done.3
  56.2 5.0 %early.1 = (f32[56,328,128]{2,1,0:T(8,128)S(1)}, bf16[256,2048]{1,0:T(8,128)(2,1)S(1)}, s32[64]{0:T(128)S(1)}) custom-call(s32[1]{0:T(128)} %bitcast.h_ref, s32[16]{0:T(128)S(1)} %copy-done.5, f32[2,32,8,8,128]{4,3,2,1,0:T(8,128)S(1)} %own.1.acc_ref, bf16[32,64,128]{2,1,0:T(8,128)(2,1)S(1)} %copy-done.3, bf16[33,64,128]{2,1,0:T(8,128)(2,1)S(1)} %copy-done.1, ...), custom_call_target="tpu_custom_call" | custom-call | flops 8000000 | bytes 12000000 | tf_op jit(solution)/shard_map/early/pallas_call | solution.py:292
  61.2 0.0 collective-permute-done.6.two_below
  61.2 7.6 %late.1 = (f32[56,328,128]{2,1,0:T(8,128)S(1)}, f32[32,2,16]{2,1,0:T(2,128)S(1)}) custom-call(s32[1]{0:T(128)} %bitcast.h_ref, s32[64]{0:T(128)S(1)} %get-tuple-element.19.off, f32[56,328,128]{2,1,0:T(8,128)S(1)} %get-tuple-element.20.later_in, f32[2,32,8,8,128]{4,3,2,1,0:T(8,128)S(1)} %own.1.acc_ref, ...), custom_call_target="tpu_custom_call", output_to_operand_aliasing={{0}: (2, {})} | custom-call | flops 24000000 | bytes 12000000 | tf_op jit(solution)/shard_map/late/pallas_call | solution.py:356
  68.7 15.2 %all_to_all.10 = f32[32,2,16]{2,1,0:T(2,128)S(1)} all-to-all(f32[32,2,16]{2,1,0:T(2,128)S(1)} %get-tuple-element.23), channel_id=1, replica_groups={{0,1,32,33,64,65,96,97,128,129,160,161,192,193,224,225,256,257,288,289,..., dimensions={0} | all-to-all | bytes 8192 | tf_op jit(solution)/shard_map/all_to_all | solution.py:410
  84.0 0.1 copy.12
  84.1 27.7 %all_to_all.11 = f32[16,1,2]{2,1,0:T(1,128)S(1)} all-to-all(f32[16,1,2]{2,1,0:T(1,128)S(1)} %copy.12), channel_id=1, replica_groups={{0,2,4,6,8,10,12,14,16,18,20,22,24,26,28,30},{1,3,5,7,9,11,13,15,17,19,..., dimensions={0} | all-to-all | bytes 256 | tf_op jit(solution)/shard_map/all_to_all | solution.py:411
  111.8 0.5 divide_bitcast_fusion
  (4 shorter events, 0.1 us)
Async XLA Ops:
  1.2 10.1 %collective-permute-start = (bf16[16,1024]{1,0:T(8,128)(2,1)S(1)}, bf16[16,1024]{1,0:T(8,128)(2,1)S(1)}, u32[]{:S(2)}, u32[]{:S(2)}) collective-permute-start(bf16[16,1024]{1,0:T(8,128)(2,1)S(1)} %bitcast.12), channel_id=1, source_target_pairs={{0,32},{32,64},{64,96},{96,128},{128,160},{160,192},{192,224},{224... | collective-permute-start | bytes 98312 | tf_op jit(solution)/shard_map/ppermute | solution.py:381
  5.7 6.4 %collective-permute-start.1 = (bf16[16,1024]{1,0:T(8,128)(2,1)S(1)}, bf16[16,1024]{1,0:T(8,128)(2,1)S(1)}, u32[]{:S(2)}, u32[]{:S(2)}) collective-permute-start(bf16[16,1024]{1,0:T(8,128)(2,1)S(1)} %bitcast.13), channel_id=1, source_target_pairs={{32,0},{64,32},{96,64},{128,96},{160,128},{192,160},{224,192},{256... | collective-permute-start | bytes 98312 | tf_op jit(solution)/shard_map/ppermute | solution.py:382
  11.3 0.8 copy-start.6
  12.1 0.6 copy-start.7
  19.1 18.5 %collective-permute-start.3 = (bf16[33,64,128]{2,1,0:T(8,128)(2,1)}, bf16[33,64,128]{2,1,0:T(8,128)(2,1)S(1)}, u32[]{:S(2)}, u32[]{:S(2)}) collective-permute-start(bf16[33,64,128]{2,1,0:T(8,128)(2,1)} %get-tuple-element.18), channel_id=1, source_target_pairs={{0,1},{1,0},{2,3},{3,2},{4,5},{5,4},{6,7},{7,6},{8,9},{9,8},{10,11... | collective-permute-start | bytes 1622024 | tf_op jit(solution)/shard_map/ppermute | solution.py:387
  22.7 14.8 %collective-permute-start.4 = (bf16[32,64,128]{2,1,0:T(8,128)(2,1)}, bf16[32,64,128]{2,1,0:T(8,128)(2,1)S(1)}, u32[]{:S(2)}, u32[]{:S(2)}) collective-permute-start(bf16[32,64,128]{2,1,0:T(8,128)(2,1)} %get-tuple-element.15.half0), channel_id=1, source_target_pairs={{2,0},{3,1},{4,2},{5,3},{6,4},{7,5},{8,6},{9,7},{10,8},{11,9},{12,... | collective-permute-start | bytes 1572872 | tf_op jit(solution)/shard_map/ppermute | solution.py:388
  24.0 21.1 %collective-permute-start.2 = (bf16[48,64,128]{2,1,0:T(8,128)(2,1)}, bf16[48,64,128]{2,1,0:T(8,128)(2,1)S(1)}, u32[]{:S(2)}, u32[]{:S(2)}) collective-permute-start(bf16[48,64,128]{2,1,0:T(8,128)(2,1)} %get-tuple-element.17), channel_id=1, source_target_pairs={{32,0},{64,32},{96,64},{128,96},{160,128},{192,160},{224,192},{256... | collective-permute-start | bytes 2359304 | tf_op jit(solution)/shard_map/ppermute | solution.py:390
  37.7 23.5 %collective-permute-start.6 = (bf16[48,64,128]{2,1,0:T(8,128)(2,1)S(1)}, bf16[48,64,128]{2,1,0:T(8,128)(2,1)S(1)}, u32[]{:S(2)}, u32[]{:S(2)}) collective-permute-start(bf16[48,64,128]{2,1,0:T(8,128)(2,1)S(1)} %pack.1), channel_id=1, source_target_pairs={{32,0},{64,32},{96,64},{128,96},{160,128},{192,160},{224,192},{256... | collective-permute-start | bytes 2359304 | tf_op jit(solution)/shard_map/ppermute | solution.py:392
  39.6 14.5 %collective-permute-start.5 = (bf16[33,64,128]{2,1,0:T(8,128)(2,1)}, bf16[33,64,128]{2,1,0:T(8,128)(2,1)}, u32[]{:S(2)}, u32[]{:S(2)}) collective-permute-start(bf16[33,64,128]{2,1,0:T(8,128)(2,1)} %get-tuple-element.16.half1), channel_id=1, source_target_pairs={{0,2},{1,3},{2,4},{3,5},{4,6},{5,7},{6,8},{7,9},{8,10},{9,11},{10,... | collective-permute-start | bytes 1622024 | tf_op jit(solution)/shard_map/ppermute | solution.py:389
  43.6 0.9 copy-start.4
  45.1 1.0 copy-start
  46.2 1.0 copy-start.2
  47.2 0.7 copy-start.5
  54.1 1.0 copy-start.1
  55.1 1.0 copy-start.3

commit v4 on v3

--- a/solution.py
+++ b/solution.py
@@ -1,3 +1,5 @@
+import functools
+
 import jax
 import jax.numpy as jnp
 from jax import lax
@@ -10,23 +12,14 @@
 F32, BF16 = jnp.float32, jnp.bfloat16
 VMEM = pl.BlockSpec(memory_space=pltpu.VMEM)
 SMEM = pl.BlockSpec(memory_space=pltpu.SMEM)
-HBM = pl.BlockSpec(memory_space=pltpu.HBM)
 NT = (((1,), (1,)), ((), ()))
 
 
 def correct_kernel(
-    h_ref, off_ref, up_ref, dn_ref, f_hbm, gain_hbm, couple_hbm, mask_hbm,
-    back, fwd, swap, own_up, raw, done, f_ref, gain_ref, couple_ref, mask_ref, sems,
+    off_ref, f_ref, up_ref, dn_ref, gain_ref, couple_ref, mask_ref,
+    back, fwd, swap, own_up, raw, done,
 ):
-    h = h_ref[0]
-    pairs = (
-        (f_hbm, f_ref), (gain_hbm, gain_ref), (couple_hbm, couple_ref), (mask_hbm, mask_ref)
-    )
-    copies = [pltpu.make_async_copy(a, b, sems.at[i]) for i, (a, b) in enumerate(pairs)]
-    for copy in copies:
-        copy.start()
-    for copy in copies:
-        copy.wait()
+    h = lax.rem(lax.axis_index("tm"), 2)
 
     @pl.loop(0, 16)
     def _(f):
@@ -78,26 +71,21 @@
     fwd[32], swap[32] = offs, offs
 
 
-def correct(h, off, frames, up, dn, gain, couple, mask):
+def correct(off, frames, up, dn, gain, couple, mask):
     shapes = tuple(jax.ShapeDtypeStruct((n, 64, 128), BF16) for n in (32, 33, 33, 48))
     return pl.pallas_call(
         correct_kernel,
         out_shape=shapes,
-        in_specs=[SMEM] * 2 + [VMEM] * 2 + [HBM] * 4,
+        in_specs=[SMEM] + [VMEM] * 6,
         out_specs=(VMEM,) * 4,
         scratch_shapes=[
             pltpu.VMEM((16, 8, 48, 128), F32),
             pltpu.VMEM((2 * 32 * 64, 128), F32),
-            pltpu.VMEM((16, 32, 1024), BF16),
-            pltpu.VMEM((32, 1024), F32),
-            pltpu.VMEM((32, 1024), F32),
-            pltpu.VMEM((32, 1024), jnp.int32),
-            pltpu.SemaphoreType.DMA((4,)),
         ],
         name="correct",
         cost_estimate=pl.CostEstimate(flops=4000000, bytes_accessed=3000000, transcendentals=0),
-        compiler_params=pltpu.CompilerParams(vmem_limit_bytes=63100 << 10),
-    )(h, off, up, dn, frames, gain, couple, mask)
+        compiler_params=pltpu.CompilerParams(vmem_limit_bytes=12 << 20),
+    )(off, frames, up, dn, gain, couple, mask)
 
 
 def low_half():
@@ -108,39 +96,36 @@
     return jnp.where(low, swap, pair) if odd else jnp.where(low, pair, swap)
 
 
-def table_kernel(h_ref, bins_ref, table):
-    h = h_ref[0]
+def table_kernel(role, bins_ref, table):
+    h = lax.rem(lax.axis_index("tm"), 2)
+    half = h if role == 0 else 1 - h
     bin_id = lax.broadcasted_iota(jnp.int32, (32, 128), 0)
-    for role in range(2):
-
-        @pl.loop(0, 4)
-        def _(r8, role=role):
-            half = h if role == 0 else 1 - h
-            for g in range(4):
-                lane = pl.multiple_of(half * 512 + g * 128, 128)
-                bins = bins_ref[pl.ds(pl.multiple_of(r8 * 8, 8), 8), pl.ds(lane, 128)]
-                for i in range(8):
-                    at = pl.multiple_of(role * 4096 + r8 * 1024 + i * 128, 128)
-                    hit = jnp.where(bins[i : i + 1] == bin_id, 1.0, 0.0)
-                    table[32 * g : 32 * g + 32, pl.ds(at, 128)] = hit.astype(BF16)
-
-
-def bin_table(h, bins):
+
+    @pl.loop(0, 4)
+    def _(r8):
+        for g in range(4):
+            lane = pl.multiple_of(half * 512 + g * 128, 128)
+            bins = bins_ref[pl.ds(pl.multiple_of(r8 * 8, 8), 8), pl.ds(lane, 128)]
+            for i in range(8):
+                at = pl.multiple_of(r8 * 1024 + i * 128, 128)
+                hit = jnp.where(bins[i : i + 1] == bin_id, 1.0, 0.0)
+                table[32 * g : 32 * g + 32, pl.ds(at, 128)] = hit.astype(BF16)
+
+
+def bin_table(role, bins, cost):
     return pl.pallas_call(
-        table_kernel,
-        out_shape=jax.ShapeDtypeStruct((128, 8192), BF16),
-        in_specs=[SMEM, VMEM],
+        functools.partial(table_kernel, role),
+        out_shape=jax.ShapeDtypeStruct((128, 4096), BF16),
+        in_specs=[VMEM],
         out_specs=VMEM,
         name="table",
-        cost_estimate=pl.CostEstimate(flops=1000000, bytes_accessed=2000000, transcendentals=0),
-        compiler_params=pltpu.CompilerParams(vmem_limit_bytes=6 << 20),
-    )(h, bins)
-
-
-def own_kernel(
-    h_ref, off_ref, half0, half1, below, acc_ref, work
-):
-    h = h_ref[0]
+        cost_estimate=pl.CostEstimate(flops=cost, bytes_accessed=2000000, transcendentals=0),
+        compiler_params=pltpu.CompilerParams(vmem_limit_bytes=4 << 20),
+    )(bins)
+
+
+def own_lags(half0, half1, below, off, acc_ref, work):
+    h = lax.rem(lax.axis_index("tm"), 2)
     low = low_half()
     work[:, :, 64:72, :] = jnp.zeros((2, 56, 8, 128), F32)
     for half, main in enumerate((half0, half1)):
@@ -165,25 +150,12 @@
                 for odd in range(2):
                     t = 2 * k + odd
                     now = twice(pair, swap, odd, low)
-                    row = r + off_ref[t]
+                    row = r + off[48 * h + t]
                     for j in range((16 - t) // 2):
                         at = 4 * (t + 1 + 2 * j)
                         acc[j] = acc[j] + now * work[role, row, at : at + 8, :]
             for j in range(8):
                 acc_ref[role, r, j] = acc[j]
-
-
-def own_part(h, off, half0, half1, below):
-    return pl.pallas_call(
-        own_kernel,
-        out_shape=jax.ShapeDtypeStruct((2, 32, 8, 8, 128), F32),
-        in_specs=[SMEM] * 2 + [VMEM] * 3,
-        out_specs=VMEM,
-        scratch_shapes=[pltpu.VMEM((2, 56, 72, 128), F32)],
-        name="own",
-        cost_estimate=pl.CostEstimate(flops=8000000, bytes_accessed=7000000, transcendentals=0),
-        compiler_params=pltpu.CompilerParams(vmem_limit_bytes=20 << 20),
-    )(h, off, half0, half1, below)
 
 
 def pack_kernel(other, back, two):
@@ -250,12 +222,13 @@
 
 
 def early_kernel(
-    h_ref, off_own, acc_ref, half0, half1, own_below, other, back, fwd,
-    later, sums, off, off_rows, off_read, sem,
+    half0, half1, own_below, other, back, fwd,
+    acc_ref, later, sums, off, off_rows, off_read, work, sem,
 ):
-    h = h_ref[0]
+    h = lax.rem(lax.axis_index("tm"), 2)
     off_rows[0] = other[32].astype(F32).astype(jnp.int32)
     off_rows[1] = fwd[32].astype(F32).astype(jnp.int32)
+    off_rows[2] = half1[32].astype(F32).astype(jnp.int32)
     read = pltpu.make_async_copy(off_rows, off_read, sem)
     read.start()
     at_half = [pl.multiple_of(192 * h, 64), pl.multiple_of(256 - 128 * h, 64)]
@@ -279,38 +252,45 @@
 
     read.wait()
     for k in range(16):
-        off[48 * h + k] = off_own[k]
+        off[48 * h + k] = off_read[2, 4 * k, 0]
         off[16 + k] = off_read[0, 4 * k, 0]
         off[48 - 48 * h + k] = off_read[1, 4 * k, 0]
 
+    own_lags(half0, half1, own_below, off, acc_ref, work)
+
     @pl.loop(0, EARLY)
     def _(r):
         all_lags(later, off, acc_ref, sums, r, r * 128, EARLY)
 
 
-def early_part(h, off, acc, blocks):
+def early_part(blocks):
     return pl.pallas_call(
         early_kernel,
         out_shape=(
+            jax.ShapeDtypeStruct((2, 32, 8, 8, 128), F32),
             jax.ShapeDtypeStruct((56, 328, 128), F32),
             jax.ShapeDtypeStruct((256, 2 * EARLY * 128), BF16),
             jax.ShapeDtypeStruct((64,), jnp.int32),
         ),
-        in_specs=[SMEM] * 2 + [VMEM] * 7,
-        out_specs=(VMEM, VMEM, SMEM),
+        in_specs=[VMEM] * 6,
+        out_specs=(VMEM, VMEM, VMEM, SMEM),
         scratch_shapes=[
-            pltpu.VMEM((2, 64, 128), jnp.int32),
-            pltpu.SMEM((2, 64, 128), jnp.int32),
+            pltpu.VMEM((3, 64, 128), jnp.int32),
+            pltpu.SMEM((3, 64, 128), jnp.int32),
+            pltpu.VMEM((2, 56, 72, 128), F32),
             pltpu.SemaphoreType.DMA,
         ],
         name="early",
-        cost_estimate=pl.CostEstimate(flops=8000000, bytes_accessed=12000000, transcendentals=0),
-        compiler_params=pltpu.CompilerParams(vmem_limit_bytes=16 << 20),
-    )(h, off, acc, *blocks)
-
-
-def late_kernel(h_ref, off, later_in, acc_ref, table, sums_early, two_below, later, out_ref, sums):
-    h = h_ref[0]
+        cost_estimate=pl.CostEstimate(flops=16000000, bytes_accessed=16000000, transcendentals=0),
+        compiler_params=pltpu.CompilerParams(vmem_limit_bytes=8 << 20),
+    )(*blocks)
+
+
+def late_kernel(
+    frames_total, pixels_per_bin,
+    off, later_in, acc_ref, table0, table1, sums_early, two_below, later, out_ref, sums,
+):
+    h = lax.rem(lax.axis_index("tm"), 2)
     at_back = pl.multiple_of(128 + 128 * h, 64)
 
     @pl.loop(0, 24)
@@ -328,8 +308,7 @@
     for role in range(2):
         for ref, first, count in ((sums_early, 0, EARLY), (sums, EARLY, rows)):
             left = ref[:, role * count * 128 : (role + 1) * count * 128]
-            start = role * 4096 + first * 128
-            right = table[:, start : start + count * 128]
+            right = (table0, table1)[role][:, first * 128 : (first + count) * 128]
             both = both + lax.dot_general(left, right, NT, preferred_element_type=F32)
     both = both[:128] + both[128:]
     row = lax.broadcasted_iota(jnp.int32, (128, 128), 0)
@@ -348,25 +327,27 @@
         part = lax.dot_general(
             per_q, pick_l, NT, precision=lax.Precision.HIGHEST, preferred_element_type=F32
         )
+        lag = (2 * lax.broadcasted_iota(jnp.int32, (32, 16), 1) + side + 1).astype(F32)
+        part = part / jnp.sqrt((frames_total - lag) * pixels_per_bin)
         for f in range(16):
             out_ref[2 * f + side] = part[2 * f : 2 * f + 2, :]
 
 
-def late_part(h, off, later, acc, table, sums, two_below):
+def late_part(totals, off, later, acc, table, sums, two_below):
     return pl.pallas_call(
-        late_kernel,
+        functools.partial(late_kernel, *totals),
         out_shape=(
             jax.ShapeDtypeStruct((56, 328, 128), F32),
             jax.ShapeDtypeStruct((32, 2, 16), F32),
         ),
-        in_specs=[SMEM] * 2 + [VMEM] * 5,
+        in_specs=[SMEM] + [VMEM] * 6,
         out_specs=(VMEM,) * 2,
-        input_output_aliases={2: 0},
+        input_output_aliases={1: 0},
         scratch_shapes=[pltpu.VMEM((256, 2 * (32 - EARLY) * 128), BF16)],
         name="late",
         cost_estimate=pl.CostEstimate(flops=24000000, bytes_accessed=12000000, transcendentals=0),
-        compiler_params=pltpu.CompilerParams(vmem_limit_bytes=16 << 20),
-    )(h, off, later, acc, table, sums, two_below)[1]
+        compiler_params=pltpu.CompilerParams(vmem_limit_bytes=8 << 20),
+    )(off, later, acc, *table, sums, two_below)[1]
 
 
 def device_program(frames, pixel_gain, couple, bin_index, pixel_mask, offsets):
@@ -376,24 +357,22 @@
     pair = [(i, i ^ 1) for i in range(time_count)]
     backward = [(i + 2, i) for i in range(time_count - 2)]
     forward = [(i, i + 2) for i in range(time_count - 2)]
-    h = (lax.axis_index("tm") % 2).astype(jnp.int32).reshape(1)
 
     above = lax.ppermute(frames[:, 31, :], "flow", down)
     below = lax.ppermute(frames[:, 0, :], "flow", up)
     half0, half1, swap, own_up = correct(
-        h, offsets, frames, above, below, pixel_gain, couple, pixel_mask
+        offsets, frames, above, below, pixel_gain, couple, pixel_mask
     )
-    table = bin_table(h, bin_index)
+    table0 = bin_table(0, bin_index, 12000000000)
+    table1 = bin_table(1, bin_index, 1000000)
     other = lax.ppermute(swap, "tm", pair)
     back = lax.ppermute(half0, "tm", backward)
     fwd = lax.ppermute(half1, "tm", forward)
     own_below = lax.ppermute(own_up, "flow", up)
-    acc = own_part(h, offsets, half0, half1, own_below)
     two_below = lax.ppermute(pack(other, back), "flow", up)
-    later, sums, off = early_part(
-        h, offsets, acc, (half0, half1, own_below, other, back, fwd)
-    )
-    part = late_part(h, off, later, acc, table, sums, two_below)
+    acc, later, sums, off = early_part((half0, half1, own_below, other, back, fwd))
+    totals = (16 * time_count, 32 * flow_count * 1024 / Q)
+    part = late_part(totals, off, later, acc, (table0, table1), sums, two_below)
     both = ("flow", "tm")
     planes = [
         [f * time_count + 2 * z + s for f in range(flow_count) for s in range(2)]
@@ -404,12 +383,9 @@
         for f in range(flow_count)
         for s in range(2)
     ]
-    lag = (lax.axis_index("tm") + 1).astype(F32)
-    normaliser = jnp.sqrt((16 * time_count - lag) * (32 * flow_count * 1024 / Q))
-    part, normaliser = lax.optimization_barrier((part, normaliser))
     part = lax.all_to_all(part, both, 0, 0, axis_index_groups=planes).sum(0)
     part = lax.all_to_all(part.T.reshape(16, 1, 2), both, 0, 0, axis_index_groups=lines).sum(0)
-    return part.reshape(2, 1) / normaliser
+    return part.reshape(2, 1)
 
 
 def solution(mesh):

time: 113 us -> 101 us (0.89)
  waiting for transfers between devices: 15.7 us -> 11.1 us
  Pallas kernels: 22.5 us -> 18.7 us
  blocking collectives: 42.9 us -> 40.3 us
    ppermute x1, waiting for transfers between devices: 11.6 us -> 7.16 us  [device_program(): back = lax.ppermute(half0, 'tm', backward)]
    pallas_call x5, Pallas kernels: 22.4 us -> 18.6 us  [the longest x1 7.58 us: late_part(): pl.pallas_call(functools.partial(late_kernel, *totals), out_shape=(jax.Sh...]
    ppermute x1, waiting for transfers between devices: 3.32 us -> 0.01 us  [device_program(): fwd = lax.ppermute(half1, 'tm', forward)]
    ppermute x1, waiting for transfers between devices: 0.01 us -> 2.52 us  [device_program(): two_below = lax.ppermute(pack(other, back), 'flow', up)]
    all_to_all x1, blocking collectives: 27.7 us -> 26.1 us  [device_program(): lax.all_to_all(part.T.reshape(16, 1, 2), both, 0, 0, axis_index_groups=li...]
    unnamed x18 -> x14, local copies, waits for them, and re-layouts: 6.36 us -> 5.52 us
  transfers between devices with their start and end apart: 7 -> 7, of which waited for: 3 -> 4; matrix products, arithmetic and copies ran while one was open for 0% -> 0% of each run, Pallas kernels for 8% -> 7%
where the time goes in v4:
time: 101 us
  blocking collectives  40.3 us (40%)
  starting transfers between devices  23 us (23%)
  Pallas kernels  18.7 us (19%)
  waiting for transfers between devices  11.1 us (11%)
  local copies, waits for them, and re-layouts  6.74 us (7%)
    all_to_all x1, blocking collectives, device_program(): lax.all_to_all(part.T.reshape(16, 1, 2), both, 0, 0, axis_index_groups=li...  26.1 us
    all_to_all x1, blocking collectives, device_program(): part = lax.all_to_all(part, both, 0, 0, axis_index_groups=planes).sum(0)  14.2 us
    pallas_call x1, Pallas kernels, late_part(): pl.pallas_call(functools.partial(late_kernel, *totals), out_shape=(jax.Sh...  7.58 us
    ppermute x1, waiting for transfers between devices, device_program(): back = lax.ppermute(half0, 'tm', backward)  7.16 us
    pallas_call x1, Pallas kernels, early_part(): pl.pallas_call(early_kernel, out_shape=(jax.ShapeDtypeStruct((2, 32, 8, 8...  6.81 us
    ppermute x1, starting transfers between devices, device_program(): below = lax.ppermute(frames[:, 0, :], 'flow', up)  5.54 us
    unnamed x14, local copies, waits for them, and re-layouts  5.52 us
    ppermute x1, starting transfers between devices, device_program(): above = lax.ppermute(frames[:, 31, :], 'flow', down)  4.5 us
  transfers between devices with their start and end apart: 7, of which 4 were waited for; matrix products, arithmetic and copies ran while one was open for 0% of the time, Pallas kernels for 7%

profile of v4, /device:TPU:1, one launch (start us, length us, event | category | flops | bytes accessed | tf_op | source)
XLA Modules:
  0.0 100.7 jit_solution(7280931503823904504)
XLA Ops:
  0.0 1.1 %fusion = (bf16[16,1,1024]{2,1,0:T(2,128)(2,1)S(1)}, bf16[16,1,1024]{2,1,0:T(2,128)(2,1)S(1)}) fusion(bf16[16,32,1024]{2,1,0:T(8,128)(2,1)} %f_ref.1), kind=kLoop, calls=%fused_computation.2 | loop fusion | bytes 131072 | tf_op jit(solution)/shard_map/slice | solution.py:362
  1.2 4.5 %collective-permute-start = (bf16[16,1024]{1,0:T(8,128)(2,1)S(1)}, bf16[16,1024]{1,0:T(8,128)(2,1)S(1)}, u32[]{:S(2)}, u32[]{:S(2)}) collective-permute-start(bf16[16,1024]{1,0:T(8,128)(2,1)S(1)} %bitcast.10), channel_id=1, source_target_pairs={{0,32},{32,64},{64,96},{96,128},{128,160},{160,192},{192,224},{224... | collective-permute-start | bytes 98312 | tf_op jit(solution)/shard_map/ppermute | solution.py:361
  5.7 5.5 %collective-permute-start.1 = (bf16[16,1024]{1,0:T(8,128)(2,1)S(1)}, bf16[16,1024]{1,0:T(8,128)(2,1)S(1)}, u32[]{:S(2)}, u32[]{:S(2)}) collective-permute-start(bf16[16,1024]{1,0:T(8,128)(2,1)S(1)} %bitcast.11), channel_id=1, source_target_pairs={{32,0},{64,32},{96,64},{128,96},{160,128},{192,160},{224,192},{256... | collective-permute-start | bytes 98312 | tf_op jit(solution)/shard_map/ppermute | solution.py:362
  11.2 0.0 collective-permute-done.up_ref
  11.2 0.8 collective-permute-done.1.dn_ref
  12.1 0.0 copy-start
  12.1 1.2 %copy-done = bf16[16,32,1024]{2,1,0:T(8,128)(2,1)S(1)} copy-done((bf16[16,32,1024]{2,1,0:T(8,128)(2,1)S(1)}, bf16[16,32,1024]{2,1,0:T(8,128)(2,1)}, u32[]{:S(2)}) %copy-start) | copy-done | bytes 1048600
  13.3 0.0 copy-start.2
  13.3 0.9 copy-done.2
  14.2 0.0 copy-start.3
  14.2 0.9 copy-done.3
  15.1 0.0 copy-start.4
  15.1 0.9 copy-done.4
  16.0 0.0 copy-start.5
  16.0 0.7 copy-done.5
  16.7 3.6 %correct.1 = (bf16[32,64,128]{2,1,0:T(8,128)(2,1)S(1)}, bf16[33,64,128]{2,1,0:T(8,128)(2,1)S(1)}, bf16[33,64,128]{2,1,0:T(8,128)(2,1)S(1)}, bf16[48,64,128]{2,1,0:T(8,128)(2,1)S(1)}) custom-call(s32[16]{0:T(128)S(1)} %copy-done.5, bf16[16,32,1024]{2,1,0:T(8,128)(2,1)S(1)} %copy-done, bf16[16,1024]{1,0:T(8,128)(2,1)S(1)} %collective-permute-done.up_ref, ...), custom_call_target="tpu_custom_call" | custom-call | flops 4000000 | bytes 3000000 | tf_op jit(solution)/shard_map/correct/pallas_call | solution.py:76
  20.3 3.7 %collective-permute-start.3 = (bf16[33,64,128]{2,1,0:T(8,128)(2,1)S(1)}, bf16[33,64,128]{2,1,0:T(8,128)(2,1)S(1)}, u32[]{:S(2)}, u32[]{:S(2)}) collective-permute-start(bf16[33,64,128]{2,1,0:T(8,128)(2,1)S(1)} %get-tuple-element.17), channel_id=1, source_target_pairs={{0,1},{1,0},{2,3},{3,2},{4,5},{5,4},{6,7},{7,6},{8,9},{9,8},{10,11... | collective-permute-start | bytes 1622024 | tf_op jit(solution)/shard_map/ppermute | solution.py:368
  23.9 1.3 %collective-permute-start.4 = (bf16[32,64,128]{2,1,0:T(8,128)(2,1)S(1)}, bf16[32,64,128]{2,1,0:T(8,128)(2,1)S(1)}, u32[]{:S(2)}, u32[]{:S(2)}) collective-permute-start(bf16[32,64,128]{2,1,0:T(8,128)(2,1)S(1)} %get-tuple-element.14.half0), channel_id=1, source_target_pairs={{2,0},{3,1},{4,2},{5,3},{6,4},{7,5},{8,6},{9,7},{10,8},{11,9},{12,... | collective-permute-start | bytes 1572872 | tf_op jit(solution)/shard_map/ppermute | solution.py:369
  25.2 4.2 %collective-permute-start.5 = (bf16[33,64,128]{2,1,0:T(8,128)(2,1)S(1)}, bf16[33,64,128]{2,1,0:T(8,128)(2,1)S(1)}, u32[]{:S(2)}, u32[]{:S(2)}) collective-permute-start(bf16[33,64,128]{2,1,0:T(8,128)(2,1)S(1)} %get-tuple-element.15.half1), channel_id=1, source_target_pairs={{0,2},{1,3},{2,4},{3,5},{4,6},{5,7},{6,8},{7,9},{8,10},{9,11},{10,... | collective-permute-start | bytes 1622024 | tf_op jit(solution)/shard_map/ppermute | solution.py:370
  29.5 1.9 %collective-permute-start.2 = (bf16[48,64,128]{2,1,0:T(8,128)(2,1)S(1)}, bf16[48,64,128]{2,1,0:T(8,128)(2,1)S(1)}, u32[]{:S(2)}, u32[]{:S(2)}) collective-permute-start(bf16[48,64,128]{2,1,0:T(8,128)(2,1)S(1)} %get-tuple-element.16), channel_id=1, source_target_pairs={{32,0},{64,32},{96,64},{128,96},{160,128},{192,160},{224,192},{256... | collective-permute-start | bytes 2359304 | tf_op jit(solution)/shard_map/ppermute | solution.py:371
  31.4 7.2 %collective-permute-done.4.back = bf16[32,64,128]{2,1,0:T(8,128)(2,1)S(1)} collective-permute-done((bf16[32,64,128]{2,1,0:T(8,128)(2,1)S(1)}, bf16[32,64,128]{2,1,0:T(8,128)(2,1)S(1)}, u32[]{:S(2)}, u32[]{:S(2)}) %collective-permute-start.4) | collective-permute-done | bytes 524320 | tf_op jit(solution)/shard_map/ppermute | solution.py:369
  38.5 0.0 collective-permute-done.3.other
  38.5 0.1 pack.1
  38.7 1.9 %collective-permute-start.6 = (bf16[48,64,128]{2,1,0:T(8,128)(2,1)S(1)}, bf16[48,64,128]{2,1,0:T(8,128)(2,1)S(1)}, u32[]{:S(2)}, u32[]{:S(2)}) collective-permute-start(bf16[48,64,128]{2,1,0:T(8,128)(2,1)S(1)} %pack.1), channel_id=1, source_target_pairs={{32,0},{64,32},{96,64},{128,96},{160,128},{192,160},{224,192},{256... | collective-permute-start | bytes 2359304 | tf_op jit(solution)/shard_map/ppermute | solution.py:372
  40.6 0.0 copy-start.1
  40.6 0.9 copy-done.1
  41.5 0.3 table.2.table0
  41.8 0.3 table.3.table1
  42.1 0.0 collective-permute-done.5.fwd
  42.1 0.6 collective-permute-done.2.own_below
  42.8 6.8 %early.1 = (f32[2,32,8,8,128]{4,3,2,1,0:T(8,128)S(1)}, f32[56,328,128]{2,1,0:T(8,128)S(1)}, bf16[256,2048]{1,0:T(8,128)(2,1)S(1)}, s32[64]{0:T(128)S(1)}) custom-call(bf16[32,64,128]{2,1,0:T(8,128)(2,1)S(1)} %get-tuple-element.14.half0, bf16[33,64,128]{2,1,0:T(8,128)(2,1)S(1)} %get-tuple-element.15.half1, ...), custom_call_target="tpu_custom_call" | custom-call | flops 16000000 | bytes 16000000 | tf_op jit(solution)/shard_map/early/pallas_call | solution.py:267
  49.6 2.5 %collective-permute-done.6.two_below = bf16[48,64,128]{2,1,0:T(8,128)(2,1)S(1)} collective-permute-done((bf16[48,64,128]{2,1,0:T(8,128)(2,1)S(1)}, bf16[48,64,128]{2,1,0:T(8,128)(2,1)S(1)}, u32[]{:S(2)}, u32[]{:S(2)}) %collective-permute-start.6) | collective-permute-done | bytes 786464 | tf_op jit(solution)/shard_map/ppermute | solution.py:372
  52.1 7.6 %late.1 = (f32[56,328,128]{2,1,0:T(8,128)S(1)}, f32[32,2,16]{2,1,0:T(2,128)S(1)}) custom-call(s32[64]{0:T(128)S(1)} %get-tuple-element.18.off, f32[56,328,128]{2,1,0:T(8,128)S(1)} %get-tuple-element.19.later_in, f32[2,32,8,8,128]{4,3,2,1,0:T(8,128)S(1)} %get-tuple-element.20.acc_ref, ...), custom_call_target="tpu_custom_call", output_to_operand_aliasing={{0}: (1, {})} | custom-call | flops 24000000 | bytes 12000000 | tf_op jit(solution)/shard_map/late/pallas_call | solution.py:337
  59.7 14.2 %all_to_all.10 = f32[32,2,16]{2,1,0:T(2,128)S(1)} all-to-all(f32[32,2,16]{2,1,0:T(2,128)S(1)} %get-tuple-element.22), channel_id=1, replica_groups={{0,1,32,33,64,65,96,97,128,129,160,161,192,193,224,225,256,257,288,289,..., dimensions={0} | all-to-all | bytes 8192 | tf_op jit(solution)/shard_map/all_to_all | solution.py:386
  73.9 0.1 copy.12
  74.0 26.1 %all_to_all.11 = f32[16,1,2]{2,1,0:T(1,128)S(1)} all-to-all(f32[16,1,2]{2,1,0:T(1,128)S(1)} %copy.12), channel_id=1, replica_groups={{0,2,4,6,8,10,12,14,16,18,20,22,24,26,28,30},{1,3,5,7,9,11,13,15,17,19,..., dimensions={0} | all-to-all | bytes 256 | tf_op jit(solution)/shard_map/all_to_all | solution.py:387
  100.1 0.5 reduce_sum.19
  (3 shorter events, 0.1 us)
Async XLA Ops:
  1.2 10.1 %collective-permute-start = (bf16[16,1024]{1,0:T(8,128)(2,1)S(1)}, bf16[16,1024]{1,0:T(8,128)(2,1)S(1)}, u32[]{:S(2)}, u32[]{:S(2)}) collective-permute-start(bf16[16,1024]{1,0:T(8,128)(2,1)S(1)} %bitcast.10), channel_id=1, source_target_pairs={{0,32},{32,64},{64,96},{96,128},{128,160},{160,192},{192,224},{224... | collective-permute-start | bytes 98312 | tf_op jit(solution)/shard_map/ppermute | solution.py:361
  5.7 6.4 %collective-permute-start.1 = (bf16[16,1024]{1,0:T(8,128)(2,1)S(1)}, bf16[16,1024]{1,0:T(8,128)(2,1)S(1)}, u32[]{:S(2)}, u32[]{:S(2)}) collective-permute-start(bf16[16,1024]{1,0:T(8,128)(2,1)S(1)} %bitcast.11), channel_id=1, source_target_pairs={{32,0},{64,32},{96,64},{128,96},{160,128},{192,160},{224,192},{256... | collective-permute-start | bytes 98312 | tf_op jit(solution)/shard_map/ppermute | solution.py:362
  12.1 1.2 %copy-start = (bf16[16,32,1024]{2,1,0:T(8,128)(2,1)S(1)}, bf16[16,32,1024]{2,1,0:T(8,128)(2,1)}, u32[]{:S(2)}) copy-start(bf16[16,32,1024]{2,1,0:T(8,128)(2,1)} %f_ref.1) | copy-start | bytes 3145732
  13.3 0.9 copy-start.2
  14.2 0.9 copy-start.3
  15.1 0.9 copy-start.4
  16.0 0.7 copy-start.5
  20.3 18.3 %collective-permute-start.3 = (bf16[33,64,128]{2,1,0:T(8,128)(2,1)S(1)}, bf16[33,64,128]{2,1,0:T(8,128)(2,1)S(1)}, u32[]{:S(2)}, u32[]{:S(2)}) collective-permute-start(bf16[33,64,128]{2,1,0:T(8,128)(2,1)S(1)} %get-tuple-element.17), channel_id=1, source_target_pairs={{0,1},{1,0},{2,3},{3,2},{4,5},{5,4},{6,7},{7,6},{8,9},{9,8},{10,11... | collective-permute-start | bytes 1622024 | tf_op jit(solution)/shard_map/ppermute | solution.py:368
  23.9 14.6 %collective-permute-start.4 = (bf16[32,64,128]{2,1,0:T(8,128)(2,1)S(1)}, bf16[32,64,128]{2,1,0:T(8,128)(2,1)S(1)}, u32[]{:S(2)}, u32[]{:S(2)}) collective-permute-start(bf16[32,64,128]{2,1,0:T(8,128)(2,1)S(1)} %get-tuple-element.14.half0), channel_id=1, source_target_pairs={{2,0},{3,1},{4,2},{5,3},{6,4},{7,5},{8,6},{9,7},{10,8},{11,9},{12,... | collective-permute-start | bytes 1572872 | tf_op jit(solution)/shard_map/ppermute | solution.py:369
  25.2 16.9 %collective-permute-start.5 = (bf16[33,64,128]{2,1,0:T(8,128)(2,1)S(1)}, bf16[33,64,128]{2,1,0:T(8,128)(2,1)S(1)}, u32[]{:S(2)}, u32[]{:S(2)}) collective-permute-start(bf16[33,64,128]{2,1,0:T(8,128)(2,1)S(1)} %get-tuple-element.15.half1), channel_id=1, source_target_pairs={{0,2},{1,3},{2,4},{3,5},{4,6},{5,7},{6,8},{7,9},{8,10},{9,11},{10,... | collective-permute-start | bytes 1622024 | tf_op jit(solution)/shard_map/ppermute | solution.py:370
  29.5 13.3 %collective-permute-start.2 = (bf16[48,64,128]{2,1,0:T(8,128)(2,1)S(1)}, bf16[48,64,128]{2,1,0:T(8,128)(2,1)S(1)}, u32[]{:S(2)}, u32[]{:S(2)}) collective-permute-start(bf16[48,64,128]{2,1,0:T(8,128)(2,1)S(1)} %get-tuple-element.16), channel_id=1, source_target_pairs={{32,0},{64,32},{96,64},{128,96},{160,128},{192,160},{224,192},{256... | collective-permute-start | bytes 2359304 | tf_op jit(solution)/shard_map/ppermute | solution.py:371
  38.7 13.4 %collective-permute-start.6 = (bf16[48,64,128]{2,1,0:T(8,128)(2,1)S(1)}, bf16[48,64,128]{2,1,0:T(8,128)(2,1)S(1)}, u32[]{:S(2)}, u32[]{:S(2)}) collective-permute-start(bf16[48,64,128]{2,1,0:T(8,128)(2,1)S(1)} %pack.1), channel_id=1, source_target_pairs={{32,0},{64,32},{96,64},{128,96},{160,128},{192,160},{224,192},{256... | collective-permute-start | bytes 2359304 | tf_op jit(solution)/shard_map/ppermute | solution.py:372
  40.6 0.9 copy-start.1
